TPU v7x, 256 devices: a whole 4x4x8 slice. The times are simulated.
256 devices in a mesh: dp: 32 (over y_lo, z, core), tp: 8 (over y_hi, x).
Axes of the slice: x: 4, y: 4 (y_hi: 2, y_lo: 2; y = y_hi * 2 + y_lo), z: 8, core: 2. Of those that a mesh axis runs over, the one named last changes fastest.
Arguments:
- hidden: bfloat16 [32768, 6144], P('dp', 'tp'), may hold values from -6 to 6
- w_down: bfloat16 [2560, 6144], P('dp', 'tp'), may hold values from -0.078125 to 0.078125
- residual: bfloat16 [32768, 2560], P(('dp', 'tp')), may hold values from -15 to 15
- norm_gain: float32 [2560], replicated, may hold values from 0.5 to 1.5
- norm_bias: float32 [2560], replicated, may hold values from -3 to 3
- keep_flags: int32 [256], replicated, may hold values 0 or 1
- keep_scale: float32 [1], replicated, may hold values from 1.1 to 2
- cotangent: bfloat16 [32768, 2560], P(('dp', 'tp')), may hold values from -24 to 24
Outputs:
- mixed_rows: bfloat16 [32768, 2560], P(('dp', 'tp'))
- normed_rows: bfloat16 [32768, 2560], P('dp')
- grad_hidden: bfloat16 [32768, 6144], P('dp', 'tp')
- grad_down: float32 [2560, 6144], P('dp', 'tp')
Inputs may be any that keep to these rules, and one draw needn't show every extreme that they name: `keep_flags`: 1 keeps the image's branch, 0 drops it.
All inputs are finite; a program needn't handle non-finite values.
Results may differ from a plain program's by a relative error of at most 0.014.
Values may be sent and summed in bfloat16 or wider, within the bound.
No kernel may reach another device: no remote copies, remote signals or barrier semaphores. Data moves between devices by JAX's collectives and lax.ppermute only.
A program may use at most 128 MiB of HBM per device.

v0:
```python
import jax
import jax.numpy as jnp
from jax import lax
from jax.sharding import PartitionSpec as P

SEQ = 128


def layer_norm(values, norm_gain, norm_bias):
    row_mean = jnp.mean(values, axis=-1, keepdims=True)
    centred = values - row_mean
    row_var = jnp.mean(centred * centred, axis=-1, keepdims=True)
    return centred * lax.rsqrt(row_var + 1e-06) * norm_gain + norm_bias


def row_scales(keep_flags, keep_scale, first_row, row_count):
    row_ids = first_row + jnp.arange(row_count, dtype=jnp.int32)
    sample_ids = row_ids // SEQ
    matches = sample_ids[:, None] == jnp.arange(keep_flags.shape[0], dtype=jnp.int32)[None, :]
    kept_flag = jnp.sum(jnp.where(matches, keep_flags[None, :], 0), axis=1)
    return kept_flag.astype(jnp.float32) * keep_scale[0]


def body(hidden, w_down, residual, norm_gain, norm_bias, keep_flags, keep_scale, cotangent):
    tok_dev = residual.shape[0]
    group_rows = tok_dev * lax.axis_size("tp")
    group_start = lax.axis_index("dp") * group_rows
    own_offset = lax.axis_index("tp") * tok_dev
    own_start = group_start + own_offset
    contract_last = (((1,), (1,)), ((), ()))
    whole_down = lax.all_gather(w_down, "dp", axis=0, tiled=True)
    cot_scales = row_scales(keep_flags, keep_scale, own_start, tok_dev)
    branch_cot = (cotangent.astype(jnp.float32) * cot_scales[:, None]).astype(jnp.bfloat16)
    cot_all = lax.all_gather(branch_cot, "tp", axis=0, tiled=True)
    partial_value = lax.dot_general(
        hidden, whole_down, contract_last, preferred_element_type=jnp.float32
    )
    branch = lax.psum_scatter(
        partial_value.astype(jnp.bfloat16), "tp", scatter_dimension=0, tiled=True
    ).astype(jnp.float32)
    own_scales = row_scales(keep_flags, keep_scale, own_start, tok_dev)
    mixed_own = (residual.astype(jnp.float32) + own_scales[:, None] * branch).astype(jnp.bfloat16)
    normed = layer_norm(mixed_own.astype(jnp.float32), norm_gain, norm_bias).astype(jnp.bfloat16)
    normed_all = lax.all_gather(normed, "tp", axis=0, tiled=True)
    summed = lax.psum_scatter(
        lax.dot_general(
            cot_all, hidden, (((0,), (0,)), ((), ())), preferred_element_type=jnp.float32
        ),
        "dp",
        scatter_dimension=0,
        tiled=True,
    )
    grad_down = summed * (1.0 / keep_flags.shape[0])
    grad_hidden = jnp.dot(cot_all, whole_down, preferred_element_type=jnp.float32).astype(
        jnp.bfloat16
    )
    return (mixed_own, normed_all, grad_hidden, grad_down)


def solution(mesh):
    in_specs = (
        P("dp", "tp"),
        P("dp", "tp"),
        P(("dp", "tp"), None),
        P(),
        P(),
        P(),
        P(),
        P(("dp", "tp"), None),
    )
    out_specs = (P(("dp", "tp"), None), P("dp", None), P("dp", "tp"), P("dp", "tp"))
    return jax.shard_map(body, mesh=mesh, in_specs=in_specs, out_specs=out_specs, check_vma=False)
```

profile of v0, /device:TPU:8, one launch (start us, length us, event | category | flops | bytes accessed | tf_op | source)
XLA Modules:
  0.0 500.2 jit_solution(6713675207935606259)
XLA Ops:
  7.2 0.0 copy-start
  7.2 0.0 all-gather.4.cloned.1.call-start
  7.2 0.7 all-gather.4.cloned.1.call-update
  7.9 0.0 reduce-scatter.3.cloned.1.call-start
  8.0 71.1 %all-gather.4.cloned.1.call-done = bf16[2560,768]{1,0:T(8,128)(2,1)} async-done(((bf16[80,768]{1,0:T(8,128)(2,1)}), bf16[2560,768]{1,0:T(8,128)(2,1)}) %all-gather.4.cloned.1.call-update) | async-done | bytes 3932176 | tf_op jit(solution)/shard_map/all_gather | solution.py:31
  79.1 0.0 copy-done
  79.1 8.1 %convolution_convert_fusion = bf16[1024,2560]{1,0:T(8,128)(2,1)} fusion(bf16[1024,768]{1,0:T(8,128)(2,1)S(1)} %copy-done, bf16[2560,768]{1,0:T(8,128)(2,1)} %all-gather.4.cloned.1.call-done), kind=kOutput, calls=%fused_computation | convolution fusion | flops 4029153280 | bytes 10747904 | tf_op jit(solution)/shard_map/dot_general | solution.py:35
  87.2 0.0 copy-start.5
  87.2 0.0 copy-start.2
  87.2 0.0 copy-start.3
  87.2 0.0 reduce-scatter.3.cloned.1.call-update
  87.2 0.0 all-gather.8.cloned.1.call-start
  88.0 0.0 copy-done.5
  88.0 0.2 select_reduce_fusion
  88.2 0.5 convert_multiply_fusion
  88.7 0.0 copy-start.4
  88.7 94.7 %reduce-scatter.3.cloned.1.call-done = bf16[128,2560]{1,0:T(8,128)(2,1)} async-done(((bf16[1024,2560]{1,0:T(8,128)(2,1)}), bf16[128,2560]{1,0:T(8,128)(2,1)}) %reduce-scatter.3.cloned.1.call-update) | async-done | bytes 655376 | tf_op jit(solution)/shard_map/reduce_scatter | solution.py:38
  183.4 0.0 copy-done.2
  183.4 0.0 copy-done.3
  183.4 2.3 convert_reduce_fusion
  185.7 0.0 copy-start.1
  185.7 0.0 all-gather.8.cloned.1.call-update
  185.7 0.0 all-gather.6.cloned.1.call-start
  185.8 0.3 fusion.2
  186.1 0.0 copy-done.4
  186.1 2.0 fusion.5
  188.2 0.0 all-gather.6.cloned.1.call-update
  188.2 0.0 copy-done.1
  188.2 0.0 reduce-scatter.5.cloned.1.call-start
  188.2 82.9 %all-gather.8.cloned.1.call-done = bf16[1024,2560]{1,0:T(8,128)(2,1)} async-done(((bf16[128,2560]{1,0:T(8,128)(2,1)}), bf16[1024,2560]{1,0:T(8,128)(2,1)}) %all-gather.8.cloned.1.call-update) | async-done | bytes 5242896 | tf_op jit(solution)/shard_map/all_gather | solution.py:34
  271.2 8.7 %fusion.6 = f32[2560,768]{1,0:T(8,128)} fusion(bf16[1024,2560]{1,0:T(8,128)(2,1)} %all-gather.8.cloned.1.call-done, bf16[1024,768]{1,0:T(8,128)(2,1)S(1)} %copy-done), kind=kOutput, calls=%fused_computation.22 | convolution fusion | flops 4026531840 | bytes 14680064 | tf_op jit(solution)/shard_map/dot_general | solution.py:46
  279.9 0.0 reduce-scatter.5.cloned.1.call-update
  279.9 78.0 %all-gather.6.cloned.1.call-done = bf16[1024,2560]{1,0:T(8,128)(2,1)} async-done(((bf16[128,2560]{1,0:T(8,128)(2,1)}), bf16[1024,2560]{1,0:T(8,128)(2,1)}) %all-gather.6.cloned.1.call-update) | async-done | bytes 5242896 | tf_op jit(solution)/shard_map/all_gather | solution.py:44
  357.9 9.0 %convolution_convert_fusion.1 = bf16[1024,768]{1,0:T(8,128)(2,1)} fusion(bf16[1024,2560]{1,0:T(8,128)(2,1)} %all-gather.8.cloned.1.call-done, bf16[2560,768]{1,0:T(8,128)(2,1)} %all-gather.4.cloned.1.call-done), kind=kOutput, calls=%fused_computation.1 | convolution fusion | flops 4027318272 | bytes 10747904 | tf_op jit(solution)/shard_map/dot_general | solution.py:54
  367.0 119.9 %reduce-scatter.5.cloned.1.call-done = f32[80,768]{1,0:T(8,128)} async-done(((f32[2560,768]{1,0:T(8,128)}), f32[80,768]{1,0:T(8,128)}) %reduce-scatter.5.cloned.1.call-update) | async-done | bytes 245776 | tf_op jit(solution)/shard_map/reduce_scatter | solution.py:45
  486.8 1.7 broadcast_multiply_fusion
  488.5 5.2 %copy.14 = bf16[1024,2560]{1,0:T(8,128)(2,1)} copy(bf16[1024,2560]{1,0:T(8,128)(2,1)} %all-gather.6.cloned.1.call-done) | data formatting | bytes 10485760
  (3 shorter events, 0.0 us)
Async XLA Ops:
  7.2 71.9 %copy-start = (bf16[1024,768]{1,0:T(8,128)(2,1)S(1)}, bf16[1024,768]{1,0:T(8,128)(2,1)}, u32[]{:S(2)}) copy-start(bf16[1024,768]{1,0:T(8,128)(2,1)} %param.8) | copy-start | bytes 4718596
  7.2 71.9 %all-gather.4.cloned.1.call-start = ((), (), s32[]{:S(2)}) async-start(), calls=%async_computation.2 | async-start | bytes 4055040 | tf_op jit(solution)/shard_map/all_gather | solution.py:31
  7.9 175.5 %reduce-scatter.3.cloned.1.call-start = ((), (), s32[]{:S(2)}) async-start(), calls=%async_computation.3 | async-start | bytes 5898240 | tf_op jit(solution)/shard_map/reduce_scatter | solution.py:38
  87.2 0.8 copy-start.5
  87.2 96.2 %copy-start.2 = (bf16[128,2560]{1,0:T(8,128)(2,1)S(1)}, bf16[128,2560]{1,0:T(8,128)(2,1)}, u32[]{:S(2)}) copy-start(bf16[128,2560]{1,0:T(8,128)(2,1)} %param.10) | copy-start | bytes 1966084
  87.2 96.2 %copy-start.3 = (bf16[128,2560]{1,0:T(8,128)(2,1)S(1)}, bf16[128,2560]{1,0:T(8,128)(2,1)}, u32[]{:S(2)}) copy-start(bf16[128,2560]{1,0:T(8,128)(2,1)} %param.15) | copy-start | bytes 1966084
  87.2 184.0 %all-gather.8.cloned.1.call-start = ((), (), s32[]{:S(2)}) async-start(), calls=%async_computation.5 | async-start | bytes 5898240 | tf_op jit(solution)/shard_map/all_gather | solution.py:34
  88.7 97.4 %copy-start.4 = (f32[2560]{0:T(1024)S(1)}, f32[2560]{0:T(1024)}, u32[]{:S(2)}) copy-start(f32[2560]{0:T(1024)} %param.12) | copy-start | bytes 30724
  185.7 2.5 copy-start.1
  185.7 172.2 %all-gather.6.cloned.1.call-start = ((), (), s32[]{:S(2)}) async-start(), calls=%async_computation.4 | async-start | bytes 5898240 | tf_op jit(solution)/shard_map/all_gather | solution.py:44
  188.2 298.6 %reduce-scatter.5.cloned.1.call-start = ((), (), s32[]{:S(2)}) async-start(), calls=%async_computation.6 | async-start | bytes 8110080 | tf_op jit(solution)/shard_map/reduce_scatter | solution.py:45
Sparse Core Ops, SparseCore 0:
  9.9 69.1 all-gather.3
  87.3 96.0 reduce-scatter.2
  186.9 84.2 all-gather.7
  274.5 83.3 all-gather.5
  360.5 126.2 reduce-scatter.4
where the time goes:
time: 501 us; the launch traced here: 500 us
  waiting for transfers between devices  447 us (89%)
  matrix products  25.9 us (5%)
  between operations  14.6 us (3%)
  other arithmetic  7.06 us (1%)
  local copies, waits for them, and re-layouts  5.21 us (1%)
    reduce_scatter x1, waiting for transfers between devices, body(): lax.psum_scatter(lax.dot_general(cot_all, hidden, (((0,), (0,)), ((), ())...  120 us
    reduce_scatter x1, waiting for transfers between devices, body(): lax.psum_scatter(partial_value.astype(jnp.bfloat16), 'tp', scatter_dimens...  94.7 us
    all_gather x1, waiting for transfers between devices, body(): cot_all = lax.all_gather(branch_cot, 'tp', axis=0, tiled=True)  82.9 us
    all_gather x1, waiting for transfers between devices, body(): normed_all = lax.all_gather(normed, 'tp', axis=0, tiled=True)  78 us
    all_gather x1, waiting for transfers between devices, body(): whole_down = lax.all_gather(w_down, 'dp', axis=0, tiled=True)  71.1 us
  transfers between devices with their start and end apart: 5, of which 5 were waited for; matrix products, arithmetic and copies ran while one was open for 4% of the time, Pallas kernels for 0%

commit v1 on v0

v1 whole, which is shorter than its diff:
```python
import jax
import jax.numpy as jnp
from jax import lax
from jax.sharding import Mesh
from jax.sharding import PartitionSpec as P

SEQ = 128
NX, NY = 4, 2
NZ = 8
F32, BF16 = jnp.float32, jnp.bfloat16

AXES = ("lo", "z", "core", "yh", "x")


def shift_x(v, s):
    return lax.ppermute(v, "x", [(i, (i + s) % NX) for i in range(NX)])


def swap(v, axis):
    return lax.ppermute(v, axis, [(0, 1), (1, 0)])


def swap_y(v):
    return swap(v, "yh")


def index(axis):
    return lax.axis_index(axis).astype(jnp.uint32)


def gather_first(own):
    return own, shift_x(own, 1), shift_x(own, -1), swap_y(own)


def cuts(rows):
    half = rows // 2
    return half, rows * 5 // 16


def send(to_right, to_left, to_side):
    return shift_x(to_right, 1), shift_x(to_left, -1), swap_y(to_side)


def gather_second(first):
    _, left, right, side = first
    h, _ = cuts(left.shape[0])
    return send(
        jnp.concatenate([side[:h], left[:h]]),
        jnp.concatenate([side[:h], right[h:]]),
        jnp.concatenate([left[h:], right[h:]]),
    )


def third_blocks(second):
    up, down, across = second
    h, q = cuts(up.shape[0])
    return up[:q], across[h : h + q], jnp.concatenate([up[h + q :], down[h + q :]])


def place_first(first, place):
    for at, block in zip(((0, 0), (0, -1), (0, 1), (1, 0)), first, strict=True):
        place(*at, block)


def place_second(second, place):
    up, down, across = second
    h, _ = cuts(up.shape[0])
    place(0, 2, jnp.concatenate([up[h:], down[h:]]))
    place(1, -1, jnp.concatenate([up[:h], across[:h]]))
    place(1, 1, jnp.concatenate([down[:h], across[h:]]))


def place_third(third, place):
    far_up, far_down, far_side = third
    part = far_side.shape[0] // 2
    place(1, 2, jnp.concatenate([far_up, far_side[:part], far_down, far_side[part:]]))


class Rows:
    def __init__(self, value):
        self.value = value
        self.y, self.x = index("yh"), index("x")

    def place(self, dy, dx, block):
        zero = jnp.uint32(0)
        at = ((self.y + dy) & 1, (self.x + (dx & 3)) & 3, zero, zero)
        self.value = lax.dynamic_update_slice(self.value, block[None, None], at)


together = lax.optimization_barrier


def low_pair(w_down):
    other = swap(w_down, "lo")
    lo_first = index("lo") == 0
    return jnp.stack([jnp.where(lo_first, w_down, other), jnp.where(lo_first, other, w_down)])


def both_cores(own, far):
    core_first = index("core") == 0
    both = [jnp.where(core_first, own, far), jnp.where(core_first, far, own)]
    return jnp.stack(both, axis=2).transpose(1, 0, 2, 3, 4).reshape(-1, own.shape[-1])


def pick(v, i, axis):
    return lax.dynamic_index_in_dim(v, i, axis, keepdims=False)


def scatter_z(mine):
    rows = mine.shape[2]
    mine = mine.reshape(2, NZ * rows, -1)
    return lax.psum_scatter(mine, "z", scatter_dimension=1, tiled=True)


def scatter_low(mine):
    low = index("lo")
    return pick(mine, low, 0) + swap(pick(mine, 1 - low, 0), "lo")


def layer_norm(values, norm_gain, norm_bias):
    row_mean = jnp.mean(values, axis=-1, keepdims=True)
    centred = values - row_mean
    row_var = jnp.mean(centred * centred, axis=-1, keepdims=True)
    return centred * lax.rsqrt(row_var + 1e-06) * norm_gain + norm_bias


def add(*parts):
    total = parts[0].astype(F32)
    for part in parts[1:]:
        total = total + part.astype(F32)
    return total


def body(hidden, w_down, residual, norm_gain, norm_bias, keep_flags, keep_scale, cotangent):
    tok, width = residual.shape
    y, x, zero = index("yh"), index("x"), jnp.uint32(0)
    sample = index(AXES)
    scale = lax.dynamic_slice(keep_flags, (sample,), (1,))[0].astype(F32) * keep_scale[0]

    pair, cotangent = together((low_pair(w_down), cotangent))
    own_down = lax.all_gather(pair, "z")
    branch_cot = (cotangent.astype(F32) * scale).astype(BF16)
    first = gather_first(branch_cot)
    first, hidden, blank = together((first, hidden, jnp.zeros((), BF16)))
    cot = Rows(jnp.full((NY, NX, tok, width), blank))
    second = gather_second(first)
    place_first(first, cot.place)
    second, own_down = together((second, own_down))
    whole_down = both_cores(own_down, swap(own_down, "core"))

    blocks = hidden.reshape(NY, NX, tok, -1)

    def block(dy, dx):
        at = ((y + dy) & 1, (x + (dx & 3)) & 3, zero, zero)
        return lax.dynamic_slice(blocks, at, (1, 1) + blocks.shape[2:])[0, 0]

    middle = jnp.concatenate([block(1, 1), block(1, -1), block(0, 2)])
    near = jnp.concatenate([block(0, 1), block(0, -1), block(1, 0), block(0, 0)])
    contract_last = (((1,), (1,)), ((), ()))

    def partial(rows):
        return lax.dot_general(
            rows, whole_down, contract_last, preferred_element_type=F32
        ).astype(BF16)

    h, q = cuts(tok)
    far, second, whole_down = together((partial(block(1, 2)), second, whole_down))
    cot_right, cot_left, cot_side = third_blocks(second)
    third = send(
        jnp.concatenate([cot_right, far[:q]]),
        jnp.concatenate([cot_left, far[h : h + q]]),
        jnp.concatenate([cot_side, far[q:h], far[h + q :]]),
    )
    place_second(second, cot.place)
    p_middle, p_near = partial(middle), partial(near)
    third, p_middle, p_near, cot_most = together((third, p_middle, p_near, cot.value))
    cot.value = cot_most
    s_up, s_down, s_side = (v[v.shape[0] // 2 :] for v in third)
    p_right, p_left, p_two = (p_middle[k * tok : (k + 1) * tok] for k in range(3))
    up_in = jnp.concatenate(
        [
            add(p_right[:q], s_up).astype(BF16),
            p_right[q:h],
            p_two[:q],
            add(p_two[q:h], s_side[: h - q]).astype(BF16),
        ]
    )
    down_in = jnp.concatenate(
        [p_left[:h], p_two[h : h + q], add(p_two[h + q :], s_side[h - q :]).astype(BF16)]
    )
    across_in = jnp.concatenate(
        [add(p_left[h : h + q], s_down).astype(BF16), p_left[h + q :], p_right[h:]]
    )
    up_in, down_in, across_in, third, cot.value = together(
        (up_in, down_in, across_in, third, cot.value)
    )
    up, down, across = send(up_in, down_in, across_in)
    place_third([v[: v.shape[0] // 2] for v in third], cot.place)
    cot_all = cot.value
    grad = lax.dot_general(
        cot_all.reshape(-1, width), hidden, (((0,), (0,)), ((), ())), preferred_element_type=F32
    )
    up, down, across, p_near, grad, cot_all = together((up, down, across, p_near, grad, cot_all))
    q_right, q_left, q_side, q_own = (p_near[k * tok : (k + 1) * tok] for k in range(4))
    right_in = jnp.concatenate([add(q_right[:h], up[h:]), add(q_right[h:], across[h:])])
    left_in = jnp.concatenate(
        [q_left[:h], add(q_left[h:], down[h:], across[:h]).astype(BF16)]
    )
    side_in = jnp.concatenate([add(q_side[:h], up[:h], down[:h]).astype(BF16), q_side[h:]])
    right_in, left_in, side_in, grad = together((right_in.astype(BF16), left_in, side_in, grad))
    last = send(right_in, left_in, side_in)
    parts = grad.reshape(2, NZ, 2, w_down.shape[0], -1)
    core = index("core")
    grad_two = add(
        pick(parts, core, 2), swap(pick(parts, 1 - core, 2).astype(BF16), "core")
    )
    grad_chips = scatter_z(grad_two)
    last, cot_all = together((last, cot_all))
    branch = add(q_own, *last)
    mixed = (residual.astype(F32) + scale * branch).astype(BF16)
    normed_own = layer_norm(mixed.astype(F32), norm_gain, norm_bias).astype(BF16)
    normed_own, cot_all, whole_down = together((normed_own, cot_all, whole_down))
    first = gather_first(normed_own)
    grad_hidden = jnp.dot(
        cot_all.reshape(-1, width), whole_down, preferred_element_type=F32
    ).astype(BF16)
    first, grad_hidden, cot_all = together((first, grad_hidden, cot_all))
    normed = Rows(cot_all)
    second = gather_second(first)
    place_first(first, normed.place)
    second, grad_chips = together((second, grad_chips))
    third = send(*third_blocks(second))
    summed = scatter_low(grad_chips)
    place_second(second, normed.place)
    place_third(third, normed.place)
    normed_all = normed.value.reshape(-1, width)

    grad_down = summed * (1.0 / keep_flags.shape[0])
    return (mixed, normed_all, grad_hidden, grad_down)


def solution(mesh):
    inner = Mesh(mesh.devices.reshape(2, NZ, 2, NY, NX), AXES)
    dp, tp = AXES[:3], AXES[3:]
    in_specs = (P(dp, tp), P(dp, tp), P(AXES, None), P(), P(), P(), P(), P(AXES, None))
    out_specs = (P(AXES, None), P(dp, None), P(dp, tp), P(dp, tp))
    return jax.shard_map(body, mesh=inner, in_specs=in_specs, out_specs=out_specs, check_vma=False)
```

time: 501 us -> 197 us (0.39)
  waiting for transfers between devices: 447 us -> 78.7 us
  starting transfers between devices: 0.2 us -> 46.7 us
  local copies, waits for them, and re-layouts: 5.21 us -> 17.5 us
  other arithmetic: 7.06 us -> 18.7 us
  matrix products: 25.9 us -> 19.6 us
    all_gather x3 -> x1, waiting for transfers between devices: 232 us -> 2.02 us  [body(): own_down = lax.all_gather(pair, 'z')]
    reduce_scatter x2 -> x1, waiting for transfers between devices: 215 us -> 0.01 us  [scatter_z(): return lax.psum_scatter(mine, 'z', scatter_dimension=1, tiled=True)]
    ppermute x0 -> x28, waiting for transfers between devices: none -> 76.7 us  [the longest x16 43.1 us: shift_x(): return lax.ppermute(v, 'x', [(i, (i + s) % NX) for i in range(NX)])]
    ppermute x0 -> x28, starting transfers between devices: none -> 46.6 us  [the longest x16 25.3 us: shift_x(): return lax.ppermute(v, 'x', [(i, (i + s) % NX) for i in range(NX)])]
    dynamic_update_slice x0 -> x8, other arithmetic: none -> 7.06 us  [place(): self.value = lax.dynamic_update_slice(self.value, block[None, None], at)]
    dynamic_update_slice x0 -> x8, local copies, waits for them, and re-layouts: none -> 7.02 us  [place(): self.value = lax.dynamic_update_slice(self.value, block[None, None], at)]
    dot_general x3 -> x5, matrix products: 25.9 us -> 19.6 us  [the longest x1 7.9 us: body(): jnp.dot(cot_all.reshape(-1, width), whole_down, preferred_element_type=F32)]
  transfers between devices with their start and end apart: 5 -> 30, of which waited for: 5 -> 21; matrix products, arithmetic and copies ran while one was open for 4% -> 21% of each run, Pallas kernels for 0% -> 0%
where the time goes in v1:
time: 197 us
  waiting for transfers between devices  78.7 us (40%)
  starting transfers between devices  46.7 us (24%)
  matrix products  19.6 us (10%)
  other arithmetic  18.7 us (9%)
  local copies, waits for them, and re-layouts  17.5 us (9%)
  between operations  15.9 us (8%)
    ppermute x16, waiting for transfers between devices, shift_x(): return lax.ppermute(v, 'x', [(i, (i + s) % NX) for i in range(NX)])  43.1 us
    ppermute x12, waiting for transfers between devices, swap(): return lax.ppermute(v, axis, [(0, 1), (1, 0)])  33.6 us
    ppermute x16, starting transfers between devices, shift_x(): return lax.ppermute(v, 'x', [(i, (i + s) % NX) for i in range(NX)])  25.3 us
    ppermute x12, starting transfers between devices, swap(): return lax.ppermute(v, axis, [(0, 1), (1, 0)])  21.4 us
    dot_general x1, matrix products, body(): jnp.dot(cot_all.reshape(-1, width), whole_down, preferred_element_type=F32)  7.9 us
    dynamic_update_slice x8, other arithmetic, place(): self.value = lax.dynamic_update_slice(self.value, block[None, None], at)  7.06 us
    dynamic_update_slice x8, local copies, waits for them, and re-layouts, place(): self.value = lax.dynamic_update_slice(self.value, block[None, None], at)  7.02 us
    dot_general x1, matrix products, body(): lax.dot_general(cot_all.reshape(-1, width), hidden, (((0,), (0,)), ((), (...  6.38 us
  transfers between devices with their start and end apart: 30, of which 21 were waited for; matrix products, arithmetic and copies ran while one was open for 21% of the time, Pallas kernels for 0%

profile of v1, /device:TPU:8, one launch (start us, length us, event | category | flops | bytes accessed | tf_op | source)
XLA Modules:
  0.0 197.2 jit_solution(16242218117964526221)
XLA Ops:
  7.2 2.3 %collective-permute-start = (bf16[80,768]{1,0:T(8,128)(2,1)}, bf16[80,768]{1,0:T(8,128)(2,1)S(1)}, u32[]{:S(2)}, u32[]{:S(2)}) collective-permute-start(bf16[80,768]{1,0:T(8,128)(2,1)} %param.9), channel_id=1, source_target_pairs={{0,128},{128,0},{1,129},{129,1},{2,130},{130,2},{3,131},{131,3},{4... | collective-permute-start | bytes 368648 | tf_op jit(solution)/shard_map/ppermute | solution.py:20
  9.5 3.1 %collective-permute-done = bf16[80,768]{1,0:T(8,128)(2,1)S(1)} collective-permute-done((bf16[80,768]{1,0:T(8,128)(2,1)}, bf16[80,768]{1,0:T(8,128)(2,1)S(1)}, u32[]{:S(2)}, u32[]{:S(2)}) %collective-permute-start) | collective-permute-done | bytes 122912 | tf_op jit(solution)/shard_map/ppermute | solution.py:20
  14.3 1.3 dynamic_slice.41
  17.0 1.6 collective-permute-start.1
  18.6 1.7 collective-permute-start.2
  20.3 2.3 %collective-permute-start.3 = (bf16[128,2560]{1,0:T(8,128)(2,1)S(1)}, bf16[128,2560]{1,0:T(8,128)(2,1)S(1)}, u32[]{:S(2)}, u32[]{:S(2)}) collective-permute-start(bf16[128,2560]{1,0:T(8,128)(2,1)S(1)} %multiply_convert_fusion), channel_id=1, source_target_pairs={{0,4},{4,0},{1,5},{5,1},{2,6},{6,2},{3,7},{7,3},{8,12},{12,8},{9,1... | collective-permute-start | bytes 1966088 | tf_op jit(solution)/shard_map/ppermute | solution.py:20
  22.6 11.1 %collective-permute-done.1 = bf16[128,2560]{1,0:T(8,128)(2,1)S(1)} collective-permute-done((bf16[128,2560]{1,0:T(8,128)(2,1)S(1)}, bf16[128,2560]{1,0:T(8,128)(2,1)S(1)}, u32[]{:S(2)}, u32[]{:S(2)}) %collective-permute-start.1) | collective-permute-done | bytes 655392 | tf_op jit(solution)/shard_map/ppermute | solution.py:16
  33.9 2.9 %collective-permute-done.3 = bf16[128,2560]{1,0:T(8,128)(2,1)S(1)} collective-permute-done((bf16[128,2560]{1,0:T(8,128)(2,1)S(1)}, bf16[128,2560]{1,0:T(8,128)(2,1)S(1)}, u32[]{:S(2)}, u32[]{:S(2)}) %collective-permute-start.3) | collective-permute-done | bytes 655392 | tf_op jit(solution)/shard_map/ppermute | solution.py:20
  38.2 2.8 %collective-permute-start.5 = (bf16[128,2560]{1,0:T(8,128)(2,1)S(1)}, bf16[128,2560]{1,0:T(8,128)(2,1)}, u32[]{:S(2)}, u32[]{:S(2)}) collective-permute-start(bf16[128,2560]{1,0:T(8,128)(2,1)S(1)} %get-tuple-element.171), channel_id=1, source_target_pairs={{0,3},{1,0},{2,1},{3,2},{4,7},{5,4},{6,5},{7,6},{8,11},{9,8},{10,9... | collective-permute-start | bytes 1966088 | tf_op jit(solution)/shard_map/ppermute | solution.py:16
  41.1 2.4 %collective-permute-start.6 = (bf16[128,2560]{1,0:T(8,128)(2,1)S(1)}, bf16[128,2560]{1,0:T(8,128)(2,1)}, u32[]{:S(2)}, u32[]{:S(2)}) collective-permute-start(bf16[128,2560]{1,0:T(8,128)(2,1)S(1)} %get-tuple-element.170), channel_id=1, source_target_pairs={{0,4},{4,0},{1,5},{5,1},{2,6},{6,2},{3,7},{7,3},{8,12},{12,8},{9,1... | collective-permute-start | bytes 1966088 | tf_op jit(solution)/shard_map/ppermute | solution.py:20
  44.6 2.8 %broadcast_in_dim.55 = bf16[2,4,128,2560]{3,2,1,0:T(8,128)(2,1)} broadcast(bf16[]{:T(256)} %constant.44.clone.1), dimensions={} | broadcast | bytes 5242882 | tf_op jit(solution)/shard_map/broadcast_in_dim | solution.py:145
  48.3 4.9 %collective-permute-done.4 = bf16[128,2560]{1,0:T(8,128)(2,1)S(1)} collective-permute-done((bf16[128,2560]{1,0:T(8,128)(2,1)S(1)}, bf16[128,2560]{1,0:T(8,128)(2,1)S(1)}, u32[]{:S(2)}, u32[]{:S(2)}) %collective-permute-start.4) | collective-permute-done | bytes 655392 | tf_op jit(solution)/shard_map/ppermute | solution.py:16
  53.2 3.1 %collective-permute-done.6 = bf16[128,2560]{1,0:T(8,128)(2,1)} collective-permute-done((bf16[128,2560]{1,0:T(8,128)(2,1)S(1)}, bf16[128,2560]{1,0:T(8,128)(2,1)}, u32[]{:S(2)}, u32[]{:S(2)}) %collective-permute-start.6) | collective-permute-done | bytes 655392 | tf_op jit(solution)/shard_map/ppermute | solution.py:20
  56.2 2.0 %all-gather.3.cloned.1.call-done = bf16[16,80,768]{2,1,0:T(8,128)(2,1)} async-done(((bf16[2,80,768]{2,1,0:T(8,128)(2,1)}), bf16[16,80,768]{2,1,0:T(8,128)(2,1)}) %all-gather.3.cloned.1.call-update) | async-done | bytes 1966096 | tf_op jit(solution)/shard_map/all_gather | solution.py:141
  60.9 1.5 collective-permute-done.7
  63.5 1.4 convolution_convert_fusion.2
  66.9 1.4 fusion.41
  68.3 1.5 collective-permute-start.8
  69.9 1.9 collective-permute-start.9
  71.8 2.3 %collective-permute-start.10 = (bf16[96,2560]{1,0:T(8,128)(2,1)S(1)}, bf16[96,2560]{1,0:T(8,128)(2,1)S(1)}, u32[]{:S(2)}, u32[]{:S(2)}) collective-permute-start(bf16[96,2560]{1,0:T(8,128)(2,1)S(1)} %pad_maximum_fusion.12), channel_id=1, source_target_pairs={{0,4},{4,0},{1,5},{5,1},{2,6},{6,2},{3,7},{7,3},{8,12},{12,8},{9,1... | collective-permute-start | bytes 1474568 | tf_op jit(solution)/shard_map/ppermute | solution.py:20
  75.9 2.2 %convolution_convert_fusion = bf16[512,2560]{1,0:T(8,128)(2,1)S(1)} fusion(bf16[2560,768]{1,0:T(8,128)(2,1)S(1)} %bitcast.102, bf16[128,768]{1,0:T(8,128)(2,1)S(1)} %copy-done.17, bf16[128,768]{1,0:T(8,128)(2,1)S(1)} %copy-done.18, bf16[128,768]{1,0:T(8,128)(2,1)S(1)} %copy-done.19, bf16[128,768]{1,0:T(8,128)(2,1)S(1)} %copy-done.16), kind=kOutput, calls=%fused_computation | convolution fusion | flops 2017722368 | bytes 7340032 | tf_op jit(solution)/shard_map/dot_general | solution.py:162
  79.1 1.7 convolution_convert_fusion.1
  81.2 5.1 %collective-permute-done.10 = bf16[96,2560]{1,0:T(8,128)(2,1)S(1)} collective-permute-done((bf16[96,2560]{1,0:T(8,128)(2,1)S(1)}, bf16[96,2560]{1,0:T(8,128)(2,1)S(1)}, u32[]{:S(2)}, u32[]{:S(2)}) %collective-permute-start.10) | collective-permute-done | bytes 491552 | tf_op jit(solution)/shard_map/ppermute | solution.py:20
  87.1 3.0 %collective-permute-start.12 = (bf16[128,2560]{1,0:T(8,128)(2,1)S(1)}, bf16[128,2560]{1,0:T(8,128)(2,1)S(1)}, u32[]{:S(2)}, u32[]{:S(2)}) collective-permute-start(bf16[128,2560]{1,0:T(8,128)(2,1)S(1)} %pad_maximum_fusion.7), channel_id=1, source_target_pairs={{0,3},{1,0},{2,1},{3,2},{4,7},{5,4},{6,5},{7,6},{8,11},{9,8},{10,9... | collective-permute-start | bytes 1966088 | tf_op jit(solution)/shard_map/ppermute | solution.py:16
  90.1 2.1 %collective-permute-start.13 = (bf16[128,2560]{1,0:T(8,128)(2,1)S(1)}, bf16[128,2560]{1,0:T(8,128)(2,1)S(1)}, u32[]{:S(2)}, u32[]{:S(2)}) collective-permute-start(bf16[128,2560]{1,0:T(8,128)(2,1)S(1)} %pad_maximum_fusion.8), channel_id=1, source_target_pairs={{0,4},{4,0},{1,5},{5,1},{2,6},{6,2},{3,7},{7,3},{8,12},{12,8},{9,1... | collective-permute-start | bytes 1966088 | tf_op jit(solution)/shard_map/ppermute | solution.py:20
  93.1 6.4 %fusion.49 = f32[2560,768]{1,0:T(8,128)S(1)} fusion(bf16[1024,2560]{1,0:T(8,128)(2,1)} %bitcast.25, bf16[1024,768]{1,0:T(8,128)(2,1)S(1)} %copy-done.5), kind=kOutput, calls=%fused_computation.116 | convolution fusion | flops 4026531840 | bytes 14680064 | tf_op jit(solution)/shard_map/dot_general | solution.py:200
  99.5 3.9 %collective-permute-done.11 = bf16[128,2560]{1,0:T(8,128)(2,1)S(1)} collective-permute-done((bf16[128,2560]{1,0:T(8,128)(2,1)S(1)}, bf16[128,2560]{1,0:T(8,128)(2,1)S(1)}, u32[]{:S(2)}, u32[]{:S(2)}) %collective-permute-start.11) | collective-permute-done | bytes 655392 | tf_op jit(solution)/shard_map/ppermute | solution.py:16
  103.3 3.0 %collective-permute-done.13 = bf16[128,2560]{1,0:T(8,128)(2,1)S(1)} collective-permute-done((bf16[128,2560]{1,0:T(8,128)(2,1)S(1)}, bf16[128,2560]{1,0:T(8,128)(2,1)S(1)}, u32[]{:S(2)}, u32[]{:S(2)}) %collective-permute-start.13) | collective-permute-done | bytes 655392 | tf_op jit(solution)/shard_map/ppermute | solution.py:20
  108.9 4.0 %collective-permute-done.23 = bf16[2,8,80,768]{3,2,1,0:T(8,128)(2,1)S(1)} collective-permute-done((bf16[2,8,80,768]{3,2,1,0:T(8,128)(2,1)S(1)}, bf16[2,8,80,768]{3,2,1,0:T(8,128)(2,1)S(1)}, u32[]{:S(2)}, u32[]{:S(2)}) %collective-permute-start.23) | collective-permute-done | bytes 1966112 | tf_op jit(solution)/shard_map/ppermute | solution.py:20
  112.8 2.4 %bitcast_add_fusion = f32[2,8,80,768]{3,2,1,0:T(8,128)} fusion(bf16[2,8,80,768]{3,2,1,0:T(8,128)(2,1)S(1)} %collective-permute-done.23, f32[2,8,2,80,768]{4,3,2,1,0:T(8,128)S(1)} %bitcast.107, u32[]{:T(128)S(6)} %convert_element_type.157), kind=kLoop, calls=%fused_computation.3 | loop fusion | flops 1966080 | bytes 9830404 | tf_op jit(solution)/shard_map/add | solution.py:130
  115.3 3.2 %collective-permute-start.15 = (bf16[128,2560]{1,0:T(8,128)(2,1)S(1)}, bf16[128,2560]{1,0:T(8,128)(2,1)}, u32[]{:S(2)}, u32[]{:S(2)}) collective-permute-start(bf16[128,2560]{1,0:T(8,128)(2,1)S(1)} %pad_maximum_fusion.10), channel_id=1, source_target_pairs={{0,3},{1,0},{2,1},{3,2},{4,7},{5,4},{6,5},{7,6},{8,11},{9,8},{10,9... | collective-permute-start | bytes 1966088 | tf_op jit(solution)/shard_map/ppermute | solution.py:16
  118.5 2.1 %collective-permute-start.16 = (bf16[128,2560]{1,0:T(8,128)(2,1)}, bf16[128,2560]{1,0:T(8,128)(2,1)}, u32[]{:S(2)}, u32[]{:S(2)}) collective-permute-start(bf16[128,2560]{1,0:T(8,128)(2,1)} %pad_maximum_fusion.11), channel_id=1, source_target_pairs={{0,4},{4,0},{1,5},{5,1},{2,6},{6,2},{3,7},{7,3},{8,12},{12,8},{9,1... | collective-permute-start | bytes 1966088 | tf_op jit(solution)/shard_map/ppermute | solution.py:20
  120.6 13.0 %collective-permute-done.14 = bf16[128,2560]{1,0:T(8,128)(2,1)} collective-permute-done((bf16[128,2560]{1,0:T(8,128)(2,1)}, bf16[128,2560]{1,0:T(8,128)(2,1)}, u32[]{:S(2)}, u32[]{:S(2)}) %collective-permute-start.14) | collective-permute-done | bytes 655392 | tf_op jit(solution)/shard_map/ppermute | solution.py:16
  133.6 3.0 %collective-permute-done.16 = bf16[128,2560]{1,0:T(8,128)(2,1)} collective-permute-done((bf16[128,2560]{1,0:T(8,128)(2,1)}, bf16[128,2560]{1,0:T(8,128)(2,1)}, u32[]{:S(2)}, u32[]{:S(2)}) %collective-permute-start.16) | collective-permute-done | bytes 655392 | tf_op jit(solution)/shard_map/ppermute | solution.py:20
  136.6 2.4 %convert_reduce_fusion = (f32[128]{0:T(128)S(1)}, bf16[128,2560]{1,0:T(8,128)(2,1)S(1)}) fusion(bf16[128,2560]{1,0:T(8,128)(2,1)} %collective-permute-done.16, bf16[128,2560]{1,0:T(8,128)(2,1)} %collective-permute-done.15, bf16[128,2560]{1,0:T(8,128)(2,1)} %collective-permute-done.14, bf16[512,2560]{1,0:T(8,128)(2,1)S(1)} %convolution_convert_fusion, ...), kind=kLoop, calls=%fused_computation.11 | loop fusion | flops 4259712 | bytes 3932676 | tf_op jit(solution)/shard_map/reduce_sum | solution.py:121
  139.9 3.2 %collective-permute-start.18 = (bf16[128,2560]{1,0:T(8,128)(2,1)S(1)}, bf16[128,2560]{1,0:T(8,128)(2,1)S(1)}, u32[]{:S(2)}, u32[]{:S(2)}) collective-permute-start(bf16[128,2560]{1,0:T(8,128)(2,1)S(1)} %fusion.6), channel_id=1, source_target_pairs={{0,3},{1,0},{2,1},{3,2},{4,7},{5,4},{6,5},{7,6},{8,11},{9,8},{10,9... | collective-permute-start | bytes 1966088 | tf_op jit(solution)/shard_map/ppermute | solution.py:16
  143.2 2.1 %collective-permute-start.19 = (bf16[128,2560]{1,0:T(8,128)(2,1)S(1)}, bf16[128,2560]{1,0:T(8,128)(2,1)S(1)}, u32[]{:S(2)}, u32[]{:S(2)}) collective-permute-start(bf16[128,2560]{1,0:T(8,128)(2,1)S(1)} %fusion.6), channel_id=1, source_target_pairs={{0,4},{4,0},{1,5},{5,1},{2,6},{6,2},{3,7},{7,3},{8,12},{12,8},{9,1... | collective-permute-start | bytes 1966088 | tf_op jit(solution)/shard_map/ppermute | solution.py:20
  145.2 7.9 %convolution_convert_fusion.3 = bf16[1024,768]{1,0:T(8,128)(2,1)} fusion(bf16[1024,2560]{1,0:T(8,128)(2,1)} %bitcast.26, bf16[2560,768]{1,0:T(8,128)(2,1)S(1)} %bitcast.104), kind=kOutput, calls=%fused_computation.9 | convolution fusion | flops 4027318272 | bytes 10747904 | tf_op jit(solution)/shard_map/dot_general | solution.py:224
  153.1 3.3 %collective-permute-done.17 = bf16[128,2560]{1,0:T(8,128)(2,1)S(1)} collective-permute-done((bf16[128,2560]{1,0:T(8,128)(2,1)S(1)}, bf16[128,2560]{1,0:T(8,128)(2,1)S(1)}, u32[]{:S(2)}, u32[]{:S(2)}) %collective-permute-start.17) | collective-permute-done | bytes 655392 | tf_op jit(solution)/shard_map/ppermute | solution.py:16
  156.5 3.0 %collective-permute-done.19 = bf16[128,2560]{1,0:T(8,128)(2,1)S(1)} collective-permute-done((bf16[128,2560]{1,0:T(8,128)(2,1)S(1)}, bf16[128,2560]{1,0:T(8,128)(2,1)S(1)}, u32[]{:S(2)}, u32[]{:S(2)}) %collective-permute-start.19) | collective-permute-done | bytes 655392 | tf_op jit(solution)/shard_map/ppermute | solution.py:20
  159.8 3.2 %collective-permute-start.21 = (bf16[128,2560]{1,0:T(8,128)(2,1)S(1)}, bf16[128,2560]{1,0:T(8,128)(2,1)S(1)}, u32[]{:S(2)}, u32[]{:S(2)}) collective-permute-start(bf16[128,2560]{1,0:T(8,128)(2,1)S(1)} %get-tuple-element.168), channel_id=1, source_target_pairs={{0,3},{1,0},{2,1},{3,2},{4,7},{5,4},{6,5},{7,6},{8,11},{9,8},{10,9... | collective-permute-start | bytes 1966088 | tf_op jit(solution)/shard_map/ppermute | solution.py:16
  163.0 2.1 %collective-permute-start.22 = (bf16[128,2560]{1,0:T(8,128)(2,1)S(1)}, bf16[128,2560]{1,0:T(8,128)(2,1)S(1)}, u32[]{:S(2)}, u32[]{:S(2)}) collective-permute-start(bf16[128,2560]{1,0:T(8,128)(2,1)S(1)} %get-tuple-element.167), channel_id=1, source_target_pairs={{0,4},{4,0},{1,5},{5,1},{2,6},{6,2},{3,7},{7,3},{8,12},{12,8},{9,1... | collective-permute-start | bytes 1966088 | tf_op jit(solution)/shard_map/ppermute | solution.py:20
  168.6 6.3 %collective-permute-done.20 = bf16[128,2560]{1,0:T(8,128)(2,1)S(1)} collective-permute-done((bf16[128,2560]{1,0:T(8,128)(2,1)S(1)}, bf16[128,2560]{1,0:T(8,128)(2,1)S(1)}, u32[]{:S(2)}, u32[]{:S(2)}) %collective-permute-start.20) | collective-permute-done | bytes 655392 | tf_op jit(solution)/shard_map/ppermute | solution.py:16
  174.9 3.0 %collective-permute-done.22 = bf16[128,2560]{1,0:T(8,128)(2,1)S(1)} collective-permute-done((bf16[128,2560]{1,0:T(8,128)(2,1)S(1)}, bf16[128,2560]{1,0:T(8,128)(2,1)S(1)}, u32[]{:S(2)}, u32[]{:S(2)}) %collective-permute-start.22) | collective-permute-done | bytes 655392 | tf_op jit(solution)/shard_map/ppermute | solution.py:20
  178.2 2.0 %collective-permute-start.25 = (bf16[48,2560]{1,0:T(8,128)(2,1)S(1)}, bf16[48,2560]{1,0:T(8,128)(2,1)S(1)}, u32[]{:S(2)}, u32[]{:S(2)}) collective-permute-start(bf16[48,2560]{1,0:T(8,128)(2,1)S(1)} %pad_maximum_fusion.16), channel_id=1, source_target_pairs={{0,4},{4,0},{1,5},{5,1},{2,6},{6,2},{3,7},{7,3},{8,12},{12,8},{9,1... | collective-permute-start | bytes 737288 | tf_op jit(solution)/shard_map/ppermute | solution.py:20
  180.5 1.7 collective-permute-start.24
  182.3 1.7 collective-permute-start.27
  186.6 2.1 %collective-permute-done.27 = f32[80,768]{1,0:T(8,128)S(1)} collective-permute-done((f32[80,768]{1,0:T(8,128)S(1)}, f32[80,768]{1,0:T(8,128)S(1)}, u32[]{:S(2)}, u32[]{:S(2)}) %collective-permute-start.27) | collective-permute-done | bytes 245792 | tf_op jit(solution)/shard_map/ppermute | solution.py:20
  (142 shorter events, 28.1 us)
Async XLA Ops:
  7.2 9.7 %copy-start.11 = (bf16[128,2560]{1,0:T(8,128)(2,1)S(1)}, bf16[128,2560]{1,0:T(8,128)(2,1)}, u32[]{:S(2)}) copy-start(bf16[128,2560]{1,0:T(8,128)(2,1)} %param.15) | copy-start | bytes 1966084
  7.2 51.1 %all-gather.3.cloned.1.call-start = ((), (), s32[]{:S(2)}) async-start(), calls=%async_computation.2 | async-start | bytes 2211840 | tf_op jit(solution)/shard_map/all_gather | solution.py:141
  7.2 5.4 %collective-permute-start = (bf16[80,768]{1,0:T(8,128)(2,1)}, bf16[80,768]{1,0:T(8,128)(2,1)S(1)}, u32[]{:S(2)}, u32[]{:S(2)}) collective-permute-start(bf16[80,768]{1,0:T(8,128)(2,1)} %param.9), channel_id=1, source_target_pairs={{0,128},{128,0},{1,129},{129,1},{2,130},{130,2},{3,131},{131,3},{4... | collective-permute-start | bytes 368648 | tf_op jit(solution)/shard_map/ppermute | solution.py:20
  14.2 163.6 %reduce-scatter.2.cloned.1.call-start = ((), (), s32[]{:S(2)}) async-start(), calls=%async_computation.1 | async-start | bytes 4423680 | tf_op jit(solution)/shard_map/reduce_scatter | solution.py:112
  17.0 16.7 %collective-permute-start.1 = (bf16[128,2560]{1,0:T(8,128)(2,1)S(1)}, bf16[128,2560]{1,0:T(8,128)(2,1)S(1)}, u32[]{:S(2)}, u32[]{:S(2)}) collective-permute-start(bf16[128,2560]{1,0:T(8,128)(2,1)S(1)} %multiply_convert_fusion), channel_id=1, source_target_pairs={{0,1},{1,2},{2,3},{3,0},{4,5},{5,6},{6,7},{7,4},{8,9},{9,10},{10,1... | collective-permute-start | bytes 1966088 | tf_op jit(solution)/shard_map/ppermute | solution.py:16
  18.6 15.3 %collective-permute-start.2 = (bf16[128,2560]{1,0:T(8,128)(2,1)S(1)}, bf16[128,2560]{1,0:T(8,128)(2,1)S(1)}, u32[]{:S(2)}, u32[]{:S(2)}) collective-permute-start(bf16[128,2560]{1,0:T(8,128)(2,1)S(1)} %multiply_convert_fusion), channel_id=1, source_target_pairs={{0,3},{1,0},{2,1},{3,2},{4,7},{5,4},{6,5},{7,6},{8,11},{9,8},{10,9... | collective-permute-start | bytes 1966088 | tf_op jit(solution)/shard_map/ppermute | solution.py:16
  20.3 16.4 %collective-permute-start.3 = (bf16[128,2560]{1,0:T(8,128)(2,1)S(1)}, bf16[128,2560]{1,0:T(8,128)(2,1)S(1)}, u32[]{:S(2)}, u32[]{:S(2)}) collective-permute-start(bf16[128,2560]{1,0:T(8,128)(2,1)S(1)} %multiply_convert_fusion), channel_id=1, source_target_pairs={{0,4},{4,0},{1,5},{5,1},{2,6},{6,2},{3,7},{7,3},{8,12},{12,8},{9,1... | collective-permute-start | bytes 1966088 | tf_op jit(solution)/shard_map/ppermute | solution.py:20
  37.6 5.9 %copy-start.4 = (bf16[1024,768]{1,0:T(8,128)(2,1)S(1)}, bf16[1024,768]{1,0:T(8,128)(2,1)}, u32[]{:S(2)}) copy-start(bf16[1024,768]{1,0:T(8,128)(2,1)} %param.8) | copy-start | bytes 4718596
  37.8 15.4 %collective-permute-start.4 = (bf16[128,2560]{1,0:T(8,128)(2,1)S(1)}, bf16[128,2560]{1,0:T(8,128)(2,1)S(1)}, u32[]{:S(2)}, u32[]{:S(2)}) collective-permute-start(bf16[128,2560]{1,0:T(8,128)(2,1)S(1)} %get-tuple-element.172), channel_id=1, source_target_pairs={{0,1},{1,2},{2,3},{3,0},{4,5},{5,6},{6,7},{7,4},{8,9},{9,10},{10,1... | collective-permute-start | bytes 1966088 | tf_op jit(solution)/shard_map/ppermute | solution.py:16
  38.2 14.9 %collective-permute-start.5 = (bf16[128,2560]{1,0:T(8,128)(2,1)S(1)}, bf16[128,2560]{1,0:T(8,128)(2,1)}, u32[]{:S(2)}, u32[]{:S(2)}) collective-permute-start(bf16[128,2560]{1,0:T(8,128)(2,1)S(1)} %get-tuple-element.171), channel_id=1, source_target_pairs={{0,3},{1,0},{2,1},{3,2},{4,7},{5,4},{6,5},{7,6},{8,11},{9,8},{10,9... | collective-permute-start | bytes 1966088 | tf_op jit(solution)/shard_map/ppermute | solution.py:16
  41.1 15.2 %collective-permute-start.6 = (bf16[128,2560]{1,0:T(8,128)(2,1)S(1)}, bf16[128,2560]{1,0:T(8,128)(2,1)}, u32[]{:S(2)}, u32[]{:S(2)}) collective-permute-start(bf16[128,2560]{1,0:T(8,128)(2,1)S(1)} %get-tuple-element.170), channel_id=1, source_target_pairs={{0,4},{4,0},{1,5},{5,1},{2,6},{6,2},{3,7},{7,3},{8,12},{12,8},{9,1... | collective-permute-start | bytes 1966088 | tf_op jit(solution)/shard_map/ppermute | solution.py:20
  48.3 10.9 %copy-start.8 = (bf16[128,2560]{1,0:T(8,128)(2,1)S(1)}, bf16[128,2560]{1,0:T(8,128)(2,1)}, u32[]{:S(2)}) copy-start(bf16[128,2560]{1,0:T(8,128)(2,1)} %copy-done.7) | copy-start | bytes 1966084
  53.2 15.1 %copy-start.6 = (bf16[128,2560]{1,0:T(8,128)(2,1)}, bf16[128,2560]{1,0:T(8,128)(2,1)S(1)}, u32[]{:S(2)}) copy-start(bf16[128,2560]{1,0:T(8,128)(2,1)S(1)} %collective-permute-done.4) | copy-start | bytes 1966084
  58.3 4.2 %collective-permute-start.7 = (bf16[8,2,80,768]{3,2,1,0:T(8,128)(2,1)}, bf16[8,2,80,768]{3,2,1,0:T(8,128)(2,1)S(1)}, u32[]{:S(2)}, u32[]{:S(2)}) collective-permute-start(bf16[8,2,80,768]{3,2,1,0:T(8,128)(2,1)} %bitcast.108), channel_id=1, source_target_pairs={{0,8},{8,0},{1,9},{9,1},{2,10},{10,2},{3,11},{11,3},{4,12},{12,4},... | collective-permute-start | bytes 5898248 | tf_op jit(solution)/shard_map/ppermute | solution.py:20
  59.1 3.3 %copy-start.3 = (bf16[16,80,768]{2,1,0:T(8,128)(2,1)S(1)}, bf16[16,80,768]{2,1,0:T(8,128)(2,1)}, u32[]{:S(2)}) copy-start(bf16[16,80,768]{2,1,0:T(8,128)(2,1)} %all-gather.3.cloned.1.call-done) | copy-start | bytes 5898244
  63.5 15.6 %copy-start = (bf16[2,8,2,80,768]{4,3,2,1,0:T(8,128)(2,1)}, bf16[2,8,2,80,768]{4,3,2,1,0:T(8,128)(2,1)S(1)}, u32[]{:S(2)}) copy-start(bf16[2,8,2,80,768]{4,3,2,1,0:T(8,128)(2,1)S(1)} %copy.14) | copy-start | bytes 11796484
  68.3 3.5 %slice-start = ((bf16[128,2560]{1,0:T(8,128)(2,1)}), bf16[24,2560]{1,0:T(8,128)(2,1)S(1)}, s32[]{:S(2)}) async-start(bf16[128,2560]{1,0:T(8,128)(2,1)} %copy-done.6), calls=%async_computation.3 | async-start | bytes 245760 | tf_op jit(solution)/shard_map/slice | solution.py:57
  68.3 12.8 %collective-permute-start.8 = (bf16[80,2560]{1,0:T(8,128)(2,1)S(1)}, bf16[80,2560]{1,0:T(8,128)(2,1)S(1)}, u32[]{:S(2)}, u32[]{:S(2)}) collective-permute-start(bf16[80,2560]{1,0:T(8,128)(2,1)S(1)} %pad_maximum_fusion.13), channel_id=1, source_target_pairs={{0,1},{1,2},{2,3},{3,0},{4,5},{5,6},{6,7},{7,4},{8,9},{9,10},{10,1... | collective-permute-start | bytes 1228808 | tf_op jit(solution)/shard_map/ppermute | solution.py:16
  69.9 11.3 %collective-permute-start.9 = (bf16[80,2560]{1,0:T(8,128)(2,1)S(1)}, bf16[80,2560]{1,0:T(8,128)(2,1)S(1)}, u32[]{:S(2)}, u32[]{:S(2)}) collective-permute-start(bf16[80,2560]{1,0:T(8,128)(2,1)S(1)} %pad_maximum_fusion.14), channel_id=1, source_target_pairs={{0,3},{1,0},{2,1},{3,2},{4,7},{5,4},{6,5},{7,6},{8,11},{9,8},{10,9... | collective-permute-start | bytes 1228808 | tf_op jit(solution)/shard_map/ppermute | solution.py:16
  71.8 4.1 %copy-start.16 = (bf16[128,768]{1,0:T(8,128)(2,1)S(1)}, bf16[128,768]{1,0:T(8,128)(2,1)}, u32[]{:S(2)}) copy-start(bf16[128,768]{1,0:T(8,128)(2,1)} %get-tuple-element.138) | copy-start | bytes 589828
  71.8 4.1 %copy-start.17 = (bf16[128,768]{1,0:T(8,128)(2,1)S(1)}, bf16[128,768]{1,0:T(8,128)(2,1)}, u32[]{:S(2)}) copy-start(bf16[128,768]{1,0:T(8,128)(2,1)} %get-tuple-element.139) | copy-start | bytes 589828
  71.8 4.1 %copy-start.18 = (bf16[128,768]{1,0:T(8,128)(2,1)S(1)}, bf16[128,768]{1,0:T(8,128)(2,1)}, u32[]{:S(2)}) copy-start(bf16[128,768]{1,0:T(8,128)(2,1)} %get-tuple-element.140) | copy-start | bytes 589828
  71.8 4.1 %copy-start.19 = (bf16[128,768]{1,0:T(8,128)(2,1)S(1)}, bf16[128,768]{1,0:T(8,128)(2,1)}, u32[]{:S(2)}) copy-start(bf16[128,768]{1,0:T(8,128)(2,1)} %get-tuple-element.141) | copy-start | bytes 589828
  71.8 14.5 %collective-permute-start.10 = (bf16[96,2560]{1,0:T(8,128)(2,1)S(1)}, bf16[96,2560]{1,0:T(8,128)(2,1)S(1)}, u32[]{:S(2)}, u32[]{:S(2)}) collective-permute-start(bf16[96,2560]{1,0:T(8,128)(2,1)S(1)} %pad_maximum_fusion.12), channel_id=1, source_target_pairs={{0,4},{4,0},{1,5},{5,1},{2,6},{6,2},{3,7},{7,3},{8,12},{12,8},{9,1... | collective-permute-start | bytes 1474568 | tf_op jit(solution)/shard_map/ppermute | solution.py:20
  75.9 3.2 %copy-start.13 = (bf16[128,768]{1,0:T(8,128)(2,1)S(1)}, bf16[128,768]{1,0:T(8,128)(2,1)}, u32[]{:S(2)}) copy-start(bf16[128,768]{1,0:T(8,128)(2,1)} %get-tuple-element.142) | copy-start | bytes 589828
  86.7 6.3 %copy-start.5 = (bf16[1024,768]{1,0:T(8,128)(2,1)S(1)}, bf16[1024,768]{1,0:T(8,128)(2,1)}, u32[]{:S(2)}) copy-start(bf16[1024,768]{1,0:T(8,128)(2,1)} %param.8) | copy-start | bytes 4718596
  86.8 16.6 %collective-permute-start.11 = (bf16[128,2560]{1,0:T(8,128)(2,1)S(1)}, bf16[128,2560]{1,0:T(8,128)(2,1)S(1)}, u32[]{:S(2)}, u32[]{:S(2)}) collective-permute-start(bf16[128,2560]{1,0:T(8,128)(2,1)S(1)} %pad_maximum_fusion.6), channel_id=1, source_target_pairs={{0,1},{1,2},{2,3},{3,0},{4,5},{5,6},{6,7},{7,4},{8,9},{9,10},{10,1... | collective-permute-start | bytes 1966088 | tf_op jit(solution)/shard_map/ppermute | solution.py:16
  87.1 16.3 %collective-permute-start.12 = (bf16[128,2560]{1,0:T(8,128)(2,1)S(1)}, bf16[128,2560]{1,0:T(8,128)(2,1)S(1)}, u32[]{:S(2)}, u32[]{:S(2)}) collective-permute-start(bf16[128,2560]{1,0:T(8,128)(2,1)S(1)} %pad_maximum_fusion.7), channel_id=1, source_target_pairs={{0,3},{1,0},{2,1},{3,2},{4,7},{5,4},{6,5},{7,6},{8,11},{9,8},{10,9... | collective-permute-start | bytes 1966088 | tf_op jit(solution)/shard_map/ppermute | solution.py:16
  90.1 16.2 %collective-permute-start.13 = (bf16[128,2560]{1,0:T(8,128)(2,1)S(1)}, bf16[128,2560]{1,0:T(8,128)(2,1)S(1)}, u32[]{:S(2)}, u32[]{:S(2)}) collective-permute-start(bf16[128,2560]{1,0:T(8,128)(2,1)S(1)} %pad_maximum_fusion.8), channel_id=1, source_target_pairs={{0,4},{4,0},{1,5},{5,1},{2,6},{6,2},{3,7},{7,3},{8,12},{12,8},{9,1... | collective-permute-start | bytes 1966088 | tf_op jit(solution)/shard_map/ppermute | solution.py:20
  108.8 4.1 %collective-permute-start.23 = (bf16[2,8,80,768]{3,2,1,0:T(8,128)(2,1)S(1)}, bf16[2,8,80,768]{3,2,1,0:T(8,128)(2,1)S(1)}, u32[]{:S(2)}, u32[]{:S(2)}) collective-permute-start(bf16[2,8,80,768]{3,2,1,0:T(8,128)(2,1)S(1)} %fusion), channel_id=1, source_target_pairs={{0,8},{8,0},{1,9},{9,1},{2,10},{10,2},{3,11},{11,3},{4,12},{12,4},... | collective-permute-start | bytes 5898248 | tf_op jit(solution)/shard_map/ppermute | solution.py:20
  115.2 18.4 %collective-permute-start.14 = (bf16[128,2560]{1,0:T(8,128)(2,1)}, bf16[128,2560]{1,0:T(8,128)(2,1)}, u32[]{:S(2)}, u32[]{:S(2)}) collective-permute-start(bf16[128,2560]{1,0:T(8,128)(2,1)} %pad_maximum_fusion.9), channel_id=1, source_target_pairs={{0,1},{1,2},{2,3},{3,0},{4,5},{5,6},{6,7},{7,4},{8,9},{9,10},{10,1... | collective-permute-start | bytes 1966088 | tf_op jit(solution)/shard_map/ppermute | solution.py:16
  115.3 18.3 %collective-permute-start.15 = (bf16[128,2560]{1,0:T(8,128)(2,1)S(1)}, bf16[128,2560]{1,0:T(8,128)(2,1)}, u32[]{:S(2)}, u32[]{:S(2)}) collective-permute-start(bf16[128,2560]{1,0:T(8,128)(2,1)S(1)} %pad_maximum_fusion.10), channel_id=1, source_target_pairs={{0,3},{1,0},{2,1},{3,2},{4,7},{5,4},{6,5},{7,6},{8,11},{9,8},{10,9... | collective-permute-start | bytes 1966088 | tf_op jit(solution)/shard_map/ppermute | solution.py:16
  118.5 18.0 %collective-permute-start.16 = (bf16[128,2560]{1,0:T(8,128)(2,1)}, bf16[128,2560]{1,0:T(8,128)(2,1)}, u32[]{:S(2)}, u32[]{:S(2)}) collective-permute-start(bf16[128,2560]{1,0:T(8,128)(2,1)} %pad_maximum_fusion.11), channel_id=1, source_target_pairs={{0,4},{4,0},{1,5},{5,1},{2,6},{6,2},{3,7},{7,3},{8,12},{12,8},{9,1... | collective-permute-start | bytes 1966088 | tf_op jit(solution)/shard_map/ppermute | solution.py:20
  120.6 18.8 %copy-start.20 = (f32[2560]{0:T(1024)S(1)}, f32[2560]{0:T(1024)}, u32[]{:S(2)}) copy-start(f32[2560]{0:T(1024)} %param.12) | copy-start | bytes 30724
  120.6 18.8 %copy-start.21 = (f32[2560]{0:T(1024)S(1)}, f32[2560]{0:T(1024)}, u32[]{:S(2)}) copy-start(f32[2560]{0:T(1024)} %param.11) | copy-start | bytes 30724
  136.6 8.7 %copy-start.1 = (bf16[2,8,2,80,768]{4,3,2,1,0:T(8,128)(2,1)S(1)}, bf16[2,8,2,80,768]{4,3,2,1,0:T(8,128)(2,1)}, u32[]{:S(2)}) copy-start(bf16[2,8,2,80,768]{4,3,2,1,0:T(8,128)(2,1)} %copy-done) | copy-start | bytes 11796484
  139.0 14.1 %copy-start.2 = (bf16[128,2560]{1,0:T(8,128)(2,1)}, bf16[128,2560]{1,0:T(8,128)(2,1)S(1)}, u32[]{:S(2)}) copy-start(bf16[128,2560]{1,0:T(8,128)(2,1)S(1)} %get-tuple-element.119) | copy-start | bytes 1966084
  139.9 16.6 %collective-permute-start.17 = (bf16[128,2560]{1,0:T(8,128)(2,1)S(1)}, bf16[128,2560]{1,0:T(8,128)(2,1)S(1)}, u32[]{:S(2)}, u32[]{:S(2)}) collective-permute-start(bf16[128,2560]{1,0:T(8,128)(2,1)S(1)} %fusion.6), channel_id=1, source_target_pairs={{0,1},{1,2},{2,3},{3,0},{4,5},{5,6},{6,7},{7,4},{8,9},{9,10},{10,1... | collective-permute-start | bytes 1966088 | tf_op jit(solution)/shard_map/ppermute | solution.py:16
  139.9 16.5 %collective-permute-start.18 = (bf16[128,2560]{1,0:T(8,128)(2,1)S(1)}, bf16[128,2560]{1,0:T(8,128)(2,1)S(1)}, u32[]{:S(2)}, u32[]{:S(2)}) collective-permute-start(bf16[128,2560]{1,0:T(8,128)(2,1)S(1)} %fusion.6), channel_id=1, source_target_pairs={{0,3},{1,0},{2,1},{3,2},{4,7},{5,4},{6,5},{7,6},{8,11},{9,8},{10,9... | collective-permute-start | bytes 1966088 | tf_op jit(solution)/shard_map/ppermute | solution.py:16
  143.2 16.3 %collective-permute-start.19 = (bf16[128,2560]{1,0:T(8,128)(2,1)S(1)}, bf16[128,2560]{1,0:T(8,128)(2,1)S(1)}, u32[]{:S(2)}, u32[]{:S(2)}) collective-permute-start(bf16[128,2560]{1,0:T(8,128)(2,1)S(1)} %fusion.6), channel_id=1, source_target_pairs={{0,4},{4,0},{1,5},{5,1},{2,6},{6,2},{3,7},{7,3},{8,12},{12,8},{9,1... | collective-permute-start | bytes 1966088 | tf_op jit(solution)/shard_map/ppermute | solution.py:20
  159.7 15.2 %collective-permute-start.20 = (bf16[128,2560]{1,0:T(8,128)(2,1)S(1)}, bf16[128,2560]{1,0:T(8,128)(2,1)S(1)}, u32[]{:S(2)}, u32[]{:S(2)}) collective-permute-start(bf16[128,2560]{1,0:T(8,128)(2,1)S(1)} %get-tuple-element.169), channel_id=1, source_target_pairs={{0,1},{1,2},{2,3},{3,0},{4,5},{5,6},{6,7},{7,4},{8,9},{9,10},{10,1... | collective-permute-start | bytes 1966088 | tf_op jit(solution)/shard_map/ppermute | solution.py:16
  159.8 15.1 %collective-permute-start.21 = (bf16[128,2560]{1,0:T(8,128)(2,1)S(1)}, bf16[128,2560]{1,0:T(8,128)(2,1)S(1)}, u32[]{:S(2)}, u32[]{:S(2)}) collective-permute-start(bf16[128,2560]{1,0:T(8,128)(2,1)S(1)} %get-tuple-element.168), channel_id=1, source_target_pairs={{0,3},{1,0},{2,1},{3,2},{4,7},{5,4},{6,5},{7,6},{8,11},{9,8},{10,9... | collective-permute-start | bytes 1966088 | tf_op jit(solution)/shard_map/ppermute | solution.py:16
  163.0 14.9 %collective-permute-start.22 = (bf16[128,2560]{1,0:T(8,128)(2,1)S(1)}, bf16[128,2560]{1,0:T(8,128)(2,1)S(1)}, u32[]{:S(2)}, u32[]{:S(2)}) collective-permute-start(bf16[128,2560]{1,0:T(8,128)(2,1)S(1)} %get-tuple-element.167), channel_id=1, source_target_pairs={{0,4},{4,0},{1,5},{5,1},{2,6},{6,2},{3,7},{7,3},{8,12},{12,8},{9,1... | collective-permute-start | bytes 1966088 | tf_op jit(solution)/shard_map/ppermute | solution.py:20
  178.0 4.2 %copy-start.12 = (f32[2,80,768]{2,1,0:T(8,128)S(1)}, f32[2,80,768]{2,1,0:T(8,128)}, u32[]{:S(2)}) copy-start(f32[2,80,768]{2,1,0:T(8,128)} %reduce-scatter.2.cloned.1.call-done) | copy-start | bytes 1474564
  178.2 8.4 %collective-permute-start.25 = (bf16[48,2560]{1,0:T(8,128)(2,1)S(1)}, bf16[48,2560]{1,0:T(8,128)(2,1)S(1)}, u32[]{:S(2)}, u32[]{:S(2)}) collective-permute-start(bf16[48,2560]{1,0:T(8,128)(2,1)S(1)} %pad_maximum_fusion.16), channel_id=1, source_target_pairs={{0,4},{4,0},{1,5},{5,1},{2,6},{6,2},{3,7},{7,3},{8,12},{12,8},{9,1... | collective-permute-start | bytes 737288 | tf_op jit(solution)/shard_map/ppermute | solution.py:20
  180.2 9.3 %collective-permute-start.26 = (bf16[40,2560]{1,0:T(8,128)(2,1)S(1)}, bf16[40,2560]{1,0:T(8,128)(2,1)S(1)}, u32[]{:S(2)}, u32[]{:S(2)}) collective-permute-start(bf16[40,2560]{1,0:T(8,128)(2,1)S(1)} %slice.290), channel_id=1, source_target_pairs={{0,3},{1,0},{2,1},{3,2},{4,7},{5,4},{6,5},{7,6},{8,11},{9,8},{10,9... | collective-permute-start | bytes 614408 | tf_op jit(solution)/shard_map/ppermute | solution.py:16
  180.5 9.0 %collective-permute-start.24 = (bf16[40,2560]{1,0:T(8,128)(2,1)S(1)}, bf16[40,2560]{1,0:T(8,128)(2,1)S(1)}, u32[]{:S(2)}, u32[]{:S(2)}) collective-permute-start(bf16[40,2560]{1,0:T(8,128)(2,1)S(1)} %slice.286), channel_id=1, source_target_pairs={{0,1},{1,2},{2,3},{3,0},{4,5},{5,6},{6,7},{7,4},{8,9},{9,10},{10,1... | collective-permute-start | bytes 614408 | tf_op jit(solution)/shard_map/ppermute | solution.py:16
  182.3 6.5 %collective-permute-start.27 = (f32[80,768]{1,0:T(8,128)S(1)}, f32[80,768]{1,0:T(8,128)S(1)}, u32[]{:S(2)}, u32[]{:S(2)}) collective-permute-start(f32[80,768]{1,0:T(8,128)S(1)} %dynamic-slice_bitcast_fusion), channel_id=1, source_target_pairs={{0,128},{128,0},{1,129},{129,1},{2,130},{130,2},{3,131},{131,3},{4... | collective-permute-start | bytes 737288 | tf_op jit(solution)/shard_map/ppermute | solution.py:20
  (5 other events, 11.9 us)
Sparse Core Ops, SparseCore 0:
  14.4 43.8 all-gather.2
  115.3 51.4 reduce-scatter.1

commit v2 on v1

--- a/solution.py
+++ b/solution.py
@@ -28,13 +28,8 @@
     return lax.axis_index(axis).astype(jnp.uint32)
 
 
-def gather_first(own):
-    return own, shift_x(own, 1), shift_x(own, -1), swap_y(own)
-
-
-def cuts(rows):
-    half = rows // 2
-    return half, rows * 5 // 16
+def gather_first(own, early):
+    return own, shift_x(own, 1), shift_x(own, -1), swap_y(own[:early])
 
 
 def send(to_right, to_left, to_side):
@@ -42,8 +37,8 @@
 
 
 def gather_second(first):
-    _, left, right, side = first
-    h, _ = cuts(left.shape[0])
+    own, left, right, side = first
+    h = own.shape[0] // 2
     return send(
         jnp.concatenate([side[:h], left[:h]]),
         jnp.concatenate([side[:h], right[h:]]),
@@ -51,29 +46,17 @@
     )
 
 
-def third_blocks(second):
-    up, down, across = second
-    h, q = cuts(up.shape[0])
-    return up[:q], across[h : h + q], jnp.concatenate([up[h + q :], down[h + q :]])
-
-
 def place_first(first, place):
-    for at, block in zip(((0, 0), (0, -1), (0, 1), (1, 0)), first, strict=True):
+    for at, block in zip(((0, 0), (0, -1), (0, 1)), first, strict=False):
         place(*at, block)
 
 
 def place_second(second, place):
     up, down, across = second
-    h, _ = cuts(up.shape[0])
+    h = up.shape[0] // 2
     place(0, 2, jnp.concatenate([up[h:], down[h:]]))
     place(1, -1, jnp.concatenate([up[:h], across[:h]]))
     place(1, 1, jnp.concatenate([down[:h], across[h:]]))
-
-
-def place_third(third, place):
-    far_up, far_down, far_side = third
-    part = far_side.shape[0] // 2
-    place(1, 2, jnp.concatenate([far_up, far_side[:part], far_down, far_side[part:]]))
 
 
 class Rows:
@@ -140,11 +123,12 @@
     pair, cotangent = together((low_pair(w_down), cotangent))
     own_down = lax.all_gather(pair, "z")
     branch_cot = (cotangent.astype(F32) * scale).astype(BF16)
-    first = gather_first(branch_cot)
+    first = gather_first(branch_cot, tok)
     first, hidden, blank = together((first, hidden, jnp.zeros((), BF16)))
     cot = Rows(jnp.full((NY, NX, tok, width), blank))
     second = gather_second(first)
     place_first(first, cot.place)
+    cot.place(1, 0, first[3])
     second, own_down = together((second, own_down))
     whole_down = both_cores(own_down, swap(own_down, "core"))
 
@@ -155,7 +139,10 @@
         return lax.dynamic_slice(blocks, at, (1, 1) + blocks.shape[2:])[0, 0]
 
     middle = jnp.concatenate([block(1, 1), block(1, -1), block(0, 2)])
-    near = jnp.concatenate([block(0, 1), block(0, -1), block(1, 0), block(0, 0)])
+    h, q, early = tok // 2, tok * 5 // 16, tok * 3 // 4
+    side_block = block(1, 0)
+    far_rows = jnp.concatenate([block(1, 2), side_block[early:]])
+    near = jnp.concatenate([block(0, 1), block(0, -1), block(0, 0), side_block[:early]])
     contract_last = (((1,), (1,)), ((), ()))
 
     def partial(rows):
@@ -163,45 +150,43 @@
             rows, whole_down, contract_last, preferred_element_type=F32
         ).astype(BF16)
 
-    h, q = cuts(tok)
-    far, second, whole_down = together((partial(block(1, 2)), second, whole_down))
-    cot_right, cot_left, cot_side = third_blocks(second)
+    far, second, whole_down = together((partial(far_rows), second, whole_down))
     third = send(
-        jnp.concatenate([cot_right, far[:q]]),
-        jnp.concatenate([cot_left, far[h : h + q]]),
-        jnp.concatenate([cot_side, far[q:h], far[h + q :]]),
+        jnp.concatenate([second[0][:h], far[:q]]),
+        jnp.concatenate([second[2][h:], far[q : 2 * q]]),
+        far[2 * q :],
     )
     place_second(second, cot.place)
     p_middle, p_near = partial(middle), partial(near)
     third, p_middle, p_near, cot_most = together((third, p_middle, p_near, cot.value))
     cot.value = cot_most
-    s_up, s_down, s_side = (v[v.shape[0] // 2 :] for v in third)
+    s_up, s_down, s_side = third[0][h:], third[1][h:], third[2][: tok - 2 * q]
     p_right, p_left, p_two = (p_middle[k * tok : (k + 1) * tok] for k in range(3))
-    up_in = jnp.concatenate(
+    up_in = jnp.concatenate([add(p_right[:q], s_up).astype(BF16), p_right[q:h], p_two[:h]])
+    down_in = jnp.concatenate(
         [
-            add(p_right[:q], s_up).astype(BF16),
-            p_right[q:h],
-            p_two[:q],
-            add(p_two[q:h], s_side[: h - q]).astype(BF16),
+            p_left[:q],
+            add(p_left[q:h], s_down[: h - q]).astype(BF16),
+            p_two[h : 2 * q],
+            add(p_two[2 * q :], s_side).astype(BF16),
         ]
     )
-    down_in = jnp.concatenate(
-        [p_left[:h], p_two[h : h + q], add(p_two[h + q :], s_side[h - q :]).astype(BF16)]
-    )
     across_in = jnp.concatenate(
-        [add(p_left[h : h + q], s_down).astype(BF16), p_left[h + q :], p_right[h:]]
+        [add(p_left[h : 2 * q], s_down[h - q :]).astype(BF16), p_left[2 * q :], p_right[h:]]
     )
     up_in, down_in, across_in, third, cot.value = together(
         (up_in, down_in, across_in, third, cot.value)
     )
     up, down, across = send(up_in, down_in, across_in)
-    place_third([v[: v.shape[0] // 2] for v in third], cot.place)
+    cot.place(1, 2, jnp.concatenate([third[0][:h], third[1][:h]]))
+    side_late = third[2][tok - 2 * q :]
     cot_all = cot.value
     grad = lax.dot_general(
         cot_all.reshape(-1, width), hidden, (((0,), (0,)), ((), ())), preferred_element_type=F32
     )
     up, down, across, p_near, grad, cot_all = together((up, down, across, p_near, grad, cot_all))
-    q_right, q_left, q_side, q_own = (p_near[k * tok : (k + 1) * tok] for k in range(4))
+    q_right, q_left, q_own = (p_near[k * tok : (k + 1) * tok] for k in range(3))
+    q_side = p_near[3 * tok :]
     right_in = jnp.concatenate([add(q_right[:h], up[h:]), add(q_right[h:], across[h:])])
     left_in = jnp.concatenate(
         [q_left[:h], add(q_left[h:], down[h:], across[:h]).astype(BF16)]
@@ -216,11 +201,11 @@
     )
     grad_chips = scatter_z(grad_two)
     last, cot_all = together((last, cot_all))
-    branch = add(q_own, *last)
+    branch = add(q_own, last[0], last[1], jnp.concatenate([last[2], side_late]))
     mixed = (residual.astype(F32) + scale * branch).astype(BF16)
     normed_own = layer_norm(mixed.astype(F32), norm_gain, norm_bias).astype(BF16)
     normed_own, cot_all, whole_down = together((normed_own, cot_all, whole_down))
-    first = gather_first(normed_own)
+    first = gather_first(normed_own, early)
     grad_hidden = jnp.dot(
         cot_all.reshape(-1, width), whole_down, preferred_element_type=F32
     ).astype(BF16)
@@ -229,10 +214,12 @@
     second = gather_second(first)
     place_first(first, normed.place)
     second, grad_chips = together((second, grad_chips))
-    third = send(*third_blocks(second))
+    up, _, across = second
+    third = send(up[:h], across[h:], first[0][early:])
     summed = scatter_low(grad_chips)
     place_second(second, normed.place)
-    place_third(third, normed.place)
+    normed.place(1, 0, jnp.concatenate([first[3], third[2]]))
+    normed.place(1, 2, jnp.concatenate([third[0], third[1]]))
     normed_all = normed.value.reshape(-1, width)
 
     grad_down = summed * (1.0 / keep_flags.shape[0])

time: 197 us -> 191 us (0.970)
  waiting for transfers between devices: 78.7 us -> 73.8 us
    ppermute x16, waiting for transfers between devices: 43.1 us -> 27.8 us  [shift_x(): return lax.ppermute(v, 'x', [(i, (i + s) % NX) for i in range(NX)])]
    ppermute x12, waiting for transfers between devices: 33.6 us -> 40.5 us  [swap(): return lax.ppermute(v, axis, [(0, 1), (1, 0)])]
    all_gather x1, waiting for transfers between devices: 2.02 us -> 5.42 us  [body(): own_down = lax.all_gather(pair, 'z')]
    dynamic_update_slice x8 -> x9, other arithmetic: 7.06 us -> 8 us  [place(): self.value = lax.dynamic_update_slice(self.value, block[None, None], at)]
    dynamic_update_slice x8 -> x7, local copies, waits for them, and re-layouts: 7.02 us -> 6.15 us  [place(): self.value = lax.dynamic_update_slice(self.value, block[None, None], at)]
  transfers between devices with their start and end apart: 30 -> 30, of which waited for: 21 -> 20; matrix products, arithmetic and copies ran while one was open for 21% -> 23% of each run, Pallas kernels for 0% -> 0%
where the time goes in v2:
time: 191 us
  waiting for transfers between devices  73.8 us (39%)
  starting transfers between devices  45.3 us (24%)
  other arithmetic  19.5 us (10%)
  matrix products  19.5 us (10%)
  local copies, waits for them, and re-layouts  17.1 us (9%)
  between operations  15.9 us (8%)
    ppermute x12, waiting for transfers between devices, swap(): return lax.ppermute(v, axis, [(0, 1), (1, 0)])  40.5 us
    ppermute x16, waiting for transfers between devices, shift_x(): return lax.ppermute(v, 'x', [(i, (i + s) % NX) for i in range(NX)])  27.8 us
    ppermute x16, starting transfers between devices, shift_x(): return lax.ppermute(v, 'x', [(i, (i + s) % NX) for i in range(NX)])  25.4 us
    ppermute x12, starting transfers between devices, swap(): return lax.ppermute(v, axis, [(0, 1), (1, 0)])  19.8 us
    dynamic_update_slice x9, other arithmetic, place(): self.value = lax.dynamic_update_slice(self.value, block[None, None], at)  8 us
    dot_general x1, matrix products, body(): jnp.dot(cot_all.reshape(-1, width), whole_down, preferred_element_type=F32)  7.9 us
    dot_general x1, matrix products, body(): lax.dot_general(cot_all.reshape(-1, width), hidden, (((0,), (0,)), ((), (...  6.38 us
    dynamic_update_slice x7, local copies, waits for them, and re-layouts, place(): self.value = lax.dynamic_update_slice(self.value, block[None, None], at)  6.15 us
  transfers between devices with their start and end apart: 30, of which 20 were waited for; matrix products, arithmetic and copies ran while one was open for 23% of the time, Pallas kernels for 0%

profile of v2, /device:TPU:8, one launch (start us, length us, event | category | flops | bytes accessed | tf_op | source)
XLA Modules:
  0.0 191.0 jit_solution(10630621656226571100)
XLA Ops:
  7.2 2.3 %collective-permute-start = (bf16[80,768]{1,0:T(8,128)(2,1)}, bf16[80,768]{1,0:T(8,128)(2,1)S(1)}, u32[]{:S(2)}, u32[]{:S(2)}) collective-permute-start(bf16[80,768]{1,0:T(8,128)(2,1)} %param.9), channel_id=1, source_target_pairs={{0,128},{128,0},{1,129},{129,1},{2,130},{130,2},{3,131},{131,3},{4... | collective-permute-start | bytes 368648 | tf_op jit(solution)/shard_map/ppermute | solution.py:20
  9.5 1.3 dynamic_slice.41
  12.6 0.9 select_bitcast_fusion.3
  14.4 1.6 collective-permute-start.1
  16.0 1.7 collective-permute-start.2
  17.7 2.3 %collective-permute-start.3 = (bf16[128,2560]{1,0:T(8,128)(2,1)S(1)}, bf16[128,2560]{1,0:T(8,128)(2,1)S(1)}, u32[]{:S(2)}, u32[]{:S(2)}) collective-permute-start(bf16[128,2560]{1,0:T(8,128)(2,1)S(1)} %multiply_convert_fusion), channel_id=1, source_target_pairs={{0,4},{4,0},{1,5},{5,1},{2,6},{6,2},{3,7},{7,3},{8,12},{12,8},{9,1... | collective-permute-start | bytes 1966088 | tf_op jit(solution)/shard_map/ppermute | solution.py:20
  20.0 11.1 %collective-permute-done.1 = bf16[128,2560]{1,0:T(8,128)(2,1)S(1)} collective-permute-done((bf16[128,2560]{1,0:T(8,128)(2,1)S(1)}, bf16[128,2560]{1,0:T(8,128)(2,1)S(1)}, u32[]{:S(2)}, u32[]{:S(2)}) %collective-permute-start.1) | collective-permute-done | bytes 655392 | tf_op jit(solution)/shard_map/ppermute | solution.py:16
  31.3 2.9 %collective-permute-done.3 = bf16[128,2560]{1,0:T(8,128)(2,1)S(1)} collective-permute-done((bf16[128,2560]{1,0:T(8,128)(2,1)S(1)}, bf16[128,2560]{1,0:T(8,128)(2,1)S(1)}, u32[]{:S(2)}, u32[]{:S(2)}) %collective-permute-start.3) | collective-permute-done | bytes 655392 | tf_op jit(solution)/shard_map/ppermute | solution.py:20
  34.9 2.8 %collective-permute-start.5 = (bf16[128,2560]{1,0:T(8,128)(2,1)S(1)}, bf16[128,2560]{1,0:T(8,128)(2,1)S(1)}, u32[]{:S(2)}, u32[]{:S(2)}) collective-permute-start(bf16[128,2560]{1,0:T(8,128)(2,1)S(1)} %get-tuple-element.157), channel_id=1, source_target_pairs={{0,3},{1,0},{2,1},{3,2},{4,7},{5,4},{6,5},{7,6},{8,11},{9,8},{10,9... | collective-permute-start | bytes 1966088 | tf_op jit(solution)/shard_map/ppermute | solution.py:16
  37.8 2.4 %collective-permute-start.6 = (bf16[128,2560]{1,0:T(8,128)(2,1)S(1)}, bf16[128,2560]{1,0:T(8,128)(2,1)}, u32[]{:S(2)}, u32[]{:S(2)}) collective-permute-start(bf16[128,2560]{1,0:T(8,128)(2,1)S(1)} %get-tuple-element.156), channel_id=1, source_target_pairs={{0,4},{4,0},{1,5},{5,1},{2,6},{6,2},{3,7},{7,3},{8,12},{12,8},{9,1... | collective-permute-start | bytes 1966088 | tf_op jit(solution)/shard_map/ppermute | solution.py:20
  40.9 1.0 dynamic-slice_bitcast_fusion.3
  41.9 2.8 %broadcast_in_dim.55 = bf16[2,4,128,2560]{3,2,1,0:T(8,128)(2,1)} broadcast(bf16[]{:T(256)} %constant.44.clone.1), dimensions={} | broadcast | bytes 5242882 | tf_op jit(solution)/shard_map/broadcast_in_dim | solution.py:128
  45.6 4.2 %collective-permute-done.4 = bf16[128,2560]{1,0:T(8,128)(2,1)S(1)} collective-permute-done((bf16[128,2560]{1,0:T(8,128)(2,1)S(1)}, bf16[128,2560]{1,0:T(8,128)(2,1)S(1)}, u32[]{:S(2)}, u32[]{:S(2)}) %collective-permute-start.4) | collective-permute-done | bytes 655392 | tf_op jit(solution)/shard_map/ppermute | solution.py:16
  50.6 2.2 %collective-permute-done.6 = bf16[128,2560]{1,0:T(8,128)(2,1)} collective-permute-done((bf16[128,2560]{1,0:T(8,128)(2,1)S(1)}, bf16[128,2560]{1,0:T(8,128)(2,1)}, u32[]{:S(2)}, u32[]{:S(2)}) %collective-permute-start.6) | collective-permute-done | bytes 655392 | tf_op jit(solution)/shard_map/ppermute | solution.py:20
  52.8 5.4 %all-gather.3.cloned.1.call-done = bf16[16,80,768]{2,1,0:T(8,128)(2,1)} async-done(((bf16[2,80,768]{2,1,0:T(8,128)(2,1)}), bf16[16,80,768]{2,1,0:T(8,128)(2,1)}) %all-gather.3.cloned.1.call-update) | async-done | bytes 1966096 | tf_op jit(solution)/shard_map/all_gather | solution.py:124
  60.9 1.5 collective-permute-done.7
  63.5 1.4 convolution_convert_fusion.2
  65.0 1.0 copy-done.11
  66.1 1.2 collective-permute-start.8
  67.3 1.2 fusion.41
  68.6 2.2 %collective-permute-start.9 = (bf16[104,2560]{1,0:T(8,128)(2,1)S(1)}, bf16[104,2560]{1,0:T(8,128)(2,1)S(1)}, u32[]{:S(2)}, u32[]{:S(2)}) collective-permute-start(bf16[104,2560]{1,0:T(8,128)(2,1)S(1)} %pad_maximum_fusion.12), channel_id=1, source_target_pairs={{0,3},{1,0},{2,1},{3,2},{4,7},{5,4},{6,5},{7,6},{8,11},{9,8},{10,9... | collective-permute-start | bytes 1597448 | tf_op jit(solution)/shard_map/ppermute | solution.py:16
  70.7 2.1 %collective-permute-start.10 = (bf16[80,2560]{1,0:T(8,128)(2,1)S(1)}, bf16[80,2560]{1,0:T(8,128)(2,1)S(1)}, u32[]{:S(2)}, u32[]{:S(2)}) collective-permute-start(bf16[80,2560]{1,0:T(8,128)(2,1)S(1)} %slice.220), channel_id=1, source_target_pairs={{0,4},{4,0},{1,5},{5,1},{2,6},{6,2},{3,7},{7,3},{8,12},{12,8},{9,1... | collective-permute-start | bytes 1228808 | tf_op jit(solution)/shard_map/ppermute | solution.py:20
  74.7 2.1 %convolution_convert_fusion = bf16[480,2560]{1,0:T(8,128)(2,1)S(1)} fusion(bf16[2560,768]{1,0:T(8,128)(2,1)S(1)} %bitcast.105, bf16[96,768]{1,0:T(8,128)(2,1)S(1)} %copy-done.19, bf16[128,768]{1,0:T(8,128)(2,1)S(1)} %copy-done.17, bf16[128,768]{1,0:T(8,128)(2,1)S(1)} %copy-done.18, bf16[128,768]{1,0:T(8,128)(2,1)S(1)} %copy-done.16), kind=kOutput, calls=%fused_computation | convolution fusion | flops 1891614720 | bytes 7127040 | tf_op jit(solution)/shard_map/dot_general | solution.py:149
  76.8 1.0 fusion.16
  77.8 1.7 convolution_convert_fusion.1
  79.5 3.7 %collective-permute-done.10 = bf16[80,2560]{1,0:T(8,128)(2,1)S(1)} collective-permute-done((bf16[80,2560]{1,0:T(8,128)(2,1)S(1)}, bf16[80,2560]{1,0:T(8,128)(2,1)S(1)}, u32[]{:S(2)}, u32[]{:S(2)}) %collective-permute-start.10) | collective-permute-done | bytes 409632 | tf_op jit(solution)/shard_map/ppermute | solution.py:20
  85.4 2.5 %collective-permute-start.12 = (bf16[128,2560]{1,0:T(8,128)(2,1)S(1)}, bf16[128,2560]{1,0:T(8,128)(2,1)S(1)}, u32[]{:S(2)}, u32[]{:S(2)}) collective-permute-start(bf16[128,2560]{1,0:T(8,128)(2,1)S(1)} %pad_maximum_fusion.7), channel_id=1, source_target_pairs={{0,3},{1,0},{2,1},{3,2},{4,7},{5,4},{6,5},{7,6},{8,11},{9,8},{10,9... | collective-permute-start | bytes 1966088 | tf_op jit(solution)/shard_map/ppermute | solution.py:16
  87.9 2.1 %collective-permute-start.13 = (bf16[128,2560]{1,0:T(8,128)(2,1)S(1)}, bf16[128,2560]{1,0:T(8,128)(2,1)S(1)}, u32[]{:S(2)}, u32[]{:S(2)}) collective-permute-start(bf16[128,2560]{1,0:T(8,128)(2,1)S(1)} %pad_maximum_fusion.8), channel_id=1, source_target_pairs={{0,4},{4,0},{1,5},{5,1},{2,6},{6,2},{3,7},{7,3},{8,12},{12,8},{9,1... | collective-permute-start | bytes 1966088 | tf_op jit(solution)/shard_map/ppermute | solution.py:20
  90.9 6.4 %fusion.45 = f32[2560,768]{1,0:T(8,128)S(1)} fusion(bf16[1024,2560]{1,0:T(8,128)(2,1)} %bitcast.26, bf16[1024,768]{1,0:T(8,128)(2,1)S(1)} %copy-done.8), kind=kOutput, calls=%fused_computation.112 | convolution fusion | flops 4026531840 | bytes 14680064 | tf_op jit(solution)/shard_map/dot_general | solution.py:184
  97.3 3.8 %collective-permute-done.11 = bf16[128,2560]{1,0:T(8,128)(2,1)S(1)} collective-permute-done((bf16[128,2560]{1,0:T(8,128)(2,1)S(1)}, bf16[128,2560]{1,0:T(8,128)(2,1)S(1)}, u32[]{:S(2)}, u32[]{:S(2)}) %collective-permute-start.11) | collective-permute-done | bytes 655392 | tf_op jit(solution)/shard_map/ppermute | solution.py:16
  101.1 3.0 %collective-permute-done.13 = bf16[128,2560]{1,0:T(8,128)(2,1)S(1)} collective-permute-done((bf16[128,2560]{1,0:T(8,128)(2,1)S(1)}, bf16[128,2560]{1,0:T(8,128)(2,1)S(1)}, u32[]{:S(2)}, u32[]{:S(2)}) %collective-permute-start.13) | collective-permute-done | bytes 655392 | tf_op jit(solution)/shard_map/ppermute | solution.py:20
  106.7 4.0 %collective-permute-done.23 = bf16[2,8,80,768]{3,2,1,0:T(8,128)(2,1)S(1)} collective-permute-done((bf16[2,8,80,768]{3,2,1,0:T(8,128)(2,1)S(1)}, bf16[2,8,80,768]{3,2,1,0:T(8,128)(2,1)S(1)}, u32[]{:S(2)}, u32[]{:S(2)}) %collective-permute-start.23) | collective-permute-done | bytes 1966112 | tf_op jit(solution)/shard_map/ppermute | solution.py:20
  110.7 2.4 %bitcast_add_fusion = f32[2,8,80,768]{3,2,1,0:T(8,128)} fusion(bf16[2,8,80,768]{3,2,1,0:T(8,128)(2,1)S(1)} %collective-permute-done.23, f32[2,8,2,80,768]{4,3,2,1,0:T(8,128)S(1)} %bitcast.110, u32[]{:T(128)S(6)} %convert_element_type.157), kind=kLoop, calls=%fused_computation.3 | loop fusion | flops 1966080 | bytes 9830404 | tf_op jit(solution)/shard_map/add | solution.py:113
  113.1 3.2 %collective-permute-start.15 = (bf16[128,2560]{1,0:T(8,128)(2,1)S(1)}, bf16[128,2560]{1,0:T(8,128)(2,1)}, u32[]{:S(2)}, u32[]{:S(2)}) collective-permute-start(bf16[128,2560]{1,0:T(8,128)(2,1)S(1)} %pad_maximum_fusion.10), channel_id=1, source_target_pairs={{0,3},{1,0},{2,1},{3,2},{4,7},{5,4},{6,5},{7,6},{8,11},{9,8},{10,9... | collective-permute-start | bytes 1966088 | tf_op jit(solution)/shard_map/ppermute | solution.py:16
  116.3 2.1 %collective-permute-start.16 = (bf16[96,2560]{1,0:T(8,128)(2,1)}, bf16[96,2560]{1,0:T(8,128)(2,1)}, u32[]{:S(2)}, u32[]{:S(2)}) collective-permute-start(bf16[96,2560]{1,0:T(8,128)(2,1)} %pad_maximum_fusion.13), channel_id=1, source_target_pairs={{0,4},{4,0},{1,5},{5,1},{2,6},{6,2},{3,7},{7,3},{8,12},{12,8},{9,1... | collective-permute-start | bytes 1474568 | tf_op jit(solution)/shard_map/ppermute | solution.py:20
  118.5 12.4 %collective-permute-done.16 = bf16[96,2560]{1,0:T(8,128)(2,1)} collective-permute-done((bf16[96,2560]{1,0:T(8,128)(2,1)}, bf16[96,2560]{1,0:T(8,128)(2,1)}, u32[]{:S(2)}, u32[]{:S(2)}) %collective-permute-start.16) | collective-permute-done | bytes 491552 | tf_op jit(solution)/shard_map/ppermute | solution.py:20
  131.4 2.4 %convert_reduce_fusion = (f32[128]{0:T(128)S(1)}, bf16[128,2560]{1,0:T(8,128)(2,1)S(1)}) fusion(bf16[32,2560]{1,0:T(8,128)(2,1)S(1)} %slice.256, bf16[96,2560]{1,0:T(8,128)(2,1)} %collective-permute-done.16, bf16[128,2560]{1,0:T(8,128)(2,1)} %collective-permute-done.15, bf16[128,2560]{1,0:T(8,128)(2,1)} %collective-permute-done.14, ...), kind=kLoop, calls=%fused_computation.11 | loop fusion | flops 5242752 | bytes 3932676 | tf_op jit(solution)/shard_map/reduce_sum | solution.py:104
  134.7 3.2 %collective-permute-start.18 = (bf16[128,2560]{1,0:T(8,128)(2,1)S(1)}, bf16[128,2560]{1,0:T(8,128)(2,1)S(1)}, u32[]{:S(2)}, u32[]{:S(2)}) collective-permute-start(bf16[128,2560]{1,0:T(8,128)(2,1)S(1)} %fusion.6), channel_id=1, source_target_pairs={{0,3},{1,0},{2,1},{3,2},{4,7},{5,4},{6,5},{7,6},{8,11},{9,8},{10,9... | collective-permute-start | bytes 1966088 | tf_op jit(solution)/shard_map/ppermute | solution.py:16
  138.0 2.2 %collective-permute-start.19 = (bf16[96,2560]{1,0:T(8,128)(2,1)S(1)}, bf16[96,2560]{1,0:T(8,128)(2,1)S(1)}, u32[]{:S(2)}, u32[]{:S(2)}) collective-permute-start(bf16[96,2560]{1,0:T(8,128)(2,1)S(1)} %slice.257), channel_id=1, source_target_pairs={{0,4},{4,0},{1,5},{5,1},{2,6},{6,2},{3,7},{7,3},{8,12},{12,8},{9,1... | collective-permute-start | bytes 1474568 | tf_op jit(solution)/shard_map/ppermute | solution.py:20
  140.2 7.9 %convolution_convert_fusion.3 = bf16[1024,768]{1,0:T(8,128)(2,1)} fusion(bf16[1024,2560]{1,0:T(8,128)(2,1)} %bitcast.27, bf16[2560,768]{1,0:T(8,128)(2,1)S(1)} %bitcast.107), kind=kOutput, calls=%fused_computation.9 | convolution fusion | flops 4027318272 | bytes 10747904 | tf_op jit(solution)/shard_map/dot_general | solution.py:209
  148.1 3.4 %collective-permute-done.19 = bf16[96,2560]{1,0:T(8,128)(2,1)S(1)} collective-permute-done((bf16[96,2560]{1,0:T(8,128)(2,1)S(1)}, bf16[96,2560]{1,0:T(8,128)(2,1)S(1)}, u32[]{:S(2)}, u32[]{:S(2)}) %collective-permute-start.19) | collective-permute-done | bytes 491552 | tf_op jit(solution)/shard_map/ppermute | solution.py:20
  152.9 2.6 %collective-permute-start.21 = (bf16[128,2560]{1,0:T(8,128)(2,1)S(1)}, bf16[128,2560]{1,0:T(8,128)(2,1)S(1)}, u32[]{:S(2)}, u32[]{:S(2)}) collective-permute-start(bf16[128,2560]{1,0:T(8,128)(2,1)S(1)} %get-tuple-element.154), channel_id=1, source_target_pairs={{0,3},{1,0},{2,1},{3,2},{4,7},{5,4},{6,5},{7,6},{8,11},{9,8},{10,9... | collective-permute-start | bytes 1966088 | tf_op jit(solution)/shard_map/ppermute | solution.py:16
  155.5 2.1 %collective-permute-start.22 = (bf16[128,2560]{1,0:T(8,128)(2,1)S(1)}, bf16[128,2560]{1,0:T(8,128)(2,1)S(1)}, u32[]{:S(2)}, u32[]{:S(2)}) collective-permute-start(bf16[128,2560]{1,0:T(8,128)(2,1)S(1)} %get-tuple-element.153), channel_id=1, source_target_pairs={{0,4},{4,0},{1,5},{5,1},{2,6},{6,2},{3,7},{7,3},{8,12},{12,8},{9,1... | collective-permute-start | bytes 1966088 | tf_op jit(solution)/shard_map/ppermute | solution.py:20
  157.6 1.5 collective-permute-start.24
  161.8 6.8 %collective-permute-done.20 = bf16[128,2560]{1,0:T(8,128)(2,1)S(1)} collective-permute-done((bf16[128,2560]{1,0:T(8,128)(2,1)S(1)}, bf16[128,2560]{1,0:T(8,128)(2,1)S(1)}, u32[]{:S(2)}, u32[]{:S(2)}) %collective-permute-start.20) | collective-permute-done | bytes 655392 | tf_op jit(solution)/shard_map/ppermute | solution.py:16
  168.6 4.7 %collective-permute-done.22 = bf16[128,2560]{1,0:T(8,128)(2,1)S(1)} collective-permute-done((bf16[128,2560]{1,0:T(8,128)(2,1)S(1)}, bf16[128,2560]{1,0:T(8,128)(2,1)S(1)}, u32[]{:S(2)}, u32[]{:S(2)}) %collective-permute-start.22) | collective-permute-done | bytes 655392 | tf_op jit(solution)/shard_map/ppermute | solution.py:20
  173.5 1.5 collective-permute-start.26
  179.8 2.2 %collective-permute-done.27 = f32[80,768]{1,0:T(8,128)S(1)} collective-permute-done((f32[80,768]{1,0:T(8,128)S(1)}, f32[80,768]{1,0:T(8,128)S(1)}, u32[]{:S(2)}, u32[]{:S(2)}) %collective-permute-start.27) | collective-permute-done | bytes 245792 | tf_op jit(solution)/shard_map/ppermute | solution.py:20
  (142 shorter events, 28.6 us)
Async XLA Ops:
  7.2 7.1 %copy-start.9 = (bf16[128,2560]{1,0:T(8,128)(2,1)S(1)}, bf16[128,2560]{1,0:T(8,128)(2,1)}, u32[]{:S(2)}) copy-start(bf16[128,2560]{1,0:T(8,128)(2,1)} %param.15) | copy-start | bytes 1966084
  7.2 51.1 %all-gather.3.cloned.1.call-start = ((), (), s32[]{:S(2)}) async-start(), calls=%async_computation.2 | async-start | bytes 2211840 | tf_op jit(solution)/shard_map/all_gather | solution.py:124
  7.2 5.4 %collective-permute-start = (bf16[80,768]{1,0:T(8,128)(2,1)}, bf16[80,768]{1,0:T(8,128)(2,1)S(1)}, u32[]{:S(2)}, u32[]{:S(2)}) collective-permute-start(bf16[80,768]{1,0:T(8,128)(2,1)} %param.9), channel_id=1, source_target_pairs={{0,128},{128,0},{1,129},{129,1},{2,130},{130,2},{3,131},{131,3},{4... | collective-permute-start | bytes 368648 | tf_op jit(solution)/shard_map/ppermute | solution.py:20
  14.2 159.1 %reduce-scatter.2.cloned.1.call-start = ((), (), s32[]{:S(2)}) async-start(), calls=%async_computation.1 | async-start | bytes 4423680 | tf_op jit(solution)/shard_map/reduce_scatter | solution.py:95
  14.4 16.7 %collective-permute-start.1 = (bf16[128,2560]{1,0:T(8,128)(2,1)S(1)}, bf16[128,2560]{1,0:T(8,128)(2,1)S(1)}, u32[]{:S(2)}, u32[]{:S(2)}) collective-permute-start(bf16[128,2560]{1,0:T(8,128)(2,1)S(1)} %multiply_convert_fusion), channel_id=1, source_target_pairs={{0,1},{1,2},{2,3},{3,0},{4,5},{5,6},{6,7},{7,4},{8,9},{9,10},{10,1... | collective-permute-start | bytes 1966088 | tf_op jit(solution)/shard_map/ppermute | solution.py:16
  16.0 15.3 %collective-permute-start.2 = (bf16[128,2560]{1,0:T(8,128)(2,1)S(1)}, bf16[128,2560]{1,0:T(8,128)(2,1)S(1)}, u32[]{:S(2)}, u32[]{:S(2)}) collective-permute-start(bf16[128,2560]{1,0:T(8,128)(2,1)S(1)} %multiply_convert_fusion), channel_id=1, source_target_pairs={{0,3},{1,0},{2,1},{3,2},{4,7},{5,4},{6,5},{7,6},{8,11},{9,8},{10,9... | collective-permute-start | bytes 1966088 | tf_op jit(solution)/shard_map/ppermute | solution.py:16
  17.7 16.4 %collective-permute-start.3 = (bf16[128,2560]{1,0:T(8,128)(2,1)S(1)}, bf16[128,2560]{1,0:T(8,128)(2,1)S(1)}, u32[]{:S(2)}, u32[]{:S(2)}) collective-permute-start(bf16[128,2560]{1,0:T(8,128)(2,1)S(1)} %multiply_convert_fusion), channel_id=1, source_target_pairs={{0,4},{4,0},{1,5},{5,1},{2,6},{6,2},{3,7},{7,3},{8,12},{12,8},{9,1... | collective-permute-start | bytes 1966088 | tf_op jit(solution)/shard_map/ppermute | solution.py:20
  34.3 5.9 %copy-start.7 = (bf16[1024,768]{1,0:T(8,128)(2,1)S(1)}, bf16[1024,768]{1,0:T(8,128)(2,1)}, u32[]{:S(2)}) copy-start(bf16[1024,768]{1,0:T(8,128)(2,1)} %param.8) | copy-start | bytes 4718596
  34.5 15.3 %collective-permute-start.4 = (bf16[128,2560]{1,0:T(8,128)(2,1)S(1)}, bf16[128,2560]{1,0:T(8,128)(2,1)S(1)}, u32[]{:S(2)}, u32[]{:S(2)}) collective-permute-start(bf16[128,2560]{1,0:T(8,128)(2,1)S(1)} %get-tuple-element.158), channel_id=1, source_target_pairs={{0,1},{1,2},{2,3},{3,0},{4,5},{5,6},{6,7},{7,4},{8,9},{9,10},{10,1... | collective-permute-start | bytes 1966088 | tf_op jit(solution)/shard_map/ppermute | solution.py:16
  34.9 14.8 %collective-permute-start.5 = (bf16[128,2560]{1,0:T(8,128)(2,1)S(1)}, bf16[128,2560]{1,0:T(8,128)(2,1)S(1)}, u32[]{:S(2)}, u32[]{:S(2)}) collective-permute-start(bf16[128,2560]{1,0:T(8,128)(2,1)S(1)} %get-tuple-element.157), channel_id=1, source_target_pairs={{0,3},{1,0},{2,1},{3,2},{4,7},{5,4},{6,5},{7,6},{8,11},{9,8},{10,9... | collective-permute-start | bytes 1966088 | tf_op jit(solution)/shard_map/ppermute | solution.py:16
  37.8 15.1 %collective-permute-start.6 = (bf16[128,2560]{1,0:T(8,128)(2,1)S(1)}, bf16[128,2560]{1,0:T(8,128)(2,1)}, u32[]{:S(2)}, u32[]{:S(2)}) collective-permute-start(bf16[128,2560]{1,0:T(8,128)(2,1)S(1)} %get-tuple-element.156), channel_id=1, source_target_pairs={{0,4},{4,0},{1,5},{5,1},{2,6},{6,2},{3,7},{7,3},{8,12},{12,8},{9,1... | collective-permute-start | bytes 1966088 | tf_op jit(solution)/shard_map/ppermute | solution.py:20
  58.3 4.2 %collective-permute-start.7 = (bf16[8,2,80,768]{3,2,1,0:T(8,128)(2,1)}, bf16[8,2,80,768]{3,2,1,0:T(8,128)(2,1)S(1)}, u32[]{:S(2)}, u32[]{:S(2)}) collective-permute-start(bf16[8,2,80,768]{3,2,1,0:T(8,128)(2,1)} %bitcast.111), channel_id=1, source_target_pairs={{0,8},{8,0},{1,9},{9,1},{2,10},{10,2},{3,11},{11,3},{4,12},{12,4},... | collective-permute-start | bytes 5898248 | tf_op jit(solution)/shard_map/ppermute | solution.py:20
  59.1 3.3 %copy-start.6 = (bf16[16,80,768]{2,1,0:T(8,128)(2,1)S(1)}, bf16[16,80,768]{2,1,0:T(8,128)(2,1)}, u32[]{:S(2)}) copy-start(bf16[16,80,768]{2,1,0:T(8,128)(2,1)} %all-gather.3.cloned.1.call-done) | copy-start | bytes 5898244
  63.5 14.3 %copy-start = (bf16[2,8,2,80,768]{4,3,2,1,0:T(8,128)(2,1)}, bf16[2,8,2,80,768]{4,3,2,1,0:T(8,128)(2,1)S(1)}, u32[]{:S(2)}) copy-start(bf16[2,8,2,80,768]{4,3,2,1,0:T(8,128)(2,1)S(1)} %copy.14) | copy-start | bytes 11796484
  66.1 17.1 %collective-permute-start.8 = (bf16[104,2560]{1,0:T(8,128)(2,1)S(1)}, bf16[104,2560]{1,0:T(8,128)(2,1)S(1)}, u32[]{:S(2)}, u32[]{:S(2)}) collective-permute-start(bf16[104,2560]{1,0:T(8,128)(2,1)S(1)} %pad_maximum_fusion.11), channel_id=1, source_target_pairs={{0,1},{1,2},{2,3},{3,0},{4,5},{5,6},{6,7},{7,4},{8,9},{9,10},{10,1... | collective-permute-start | bytes 1597448 | tf_op jit(solution)/shard_map/ppermute | solution.py:16
  68.5 6.1 %copy-start.16 = (bf16[128,768]{1,0:T(8,128)(2,1)S(1)}, bf16[128,768]{1,0:T(8,128)(2,1)}, u32[]{:S(2)}) copy-start(bf16[128,768]{1,0:T(8,128)(2,1)} %get-tuple-element.128) | copy-start | bytes 589828
  68.6 6.1 %copy-start.17 = (bf16[128,768]{1,0:T(8,128)(2,1)S(1)}, bf16[128,768]{1,0:T(8,128)(2,1)}, u32[]{:S(2)}) copy-start(bf16[128,768]{1,0:T(8,128)(2,1)} %get-tuple-element.129) | copy-start | bytes 589828
  68.6 6.1 %copy-start.18 = (bf16[128,768]{1,0:T(8,128)(2,1)S(1)}, bf16[128,768]{1,0:T(8,128)(2,1)}, u32[]{:S(2)}) copy-start(bf16[128,768]{1,0:T(8,128)(2,1)} %get-tuple-element.130) | copy-start | bytes 589828
  68.6 6.1 %copy-start.19 = (bf16[96,768]{1,0:T(8,128)(2,1)S(1)}, bf16[96,768]{1,0:T(8,128)(2,1)}, u32[]{:S(2)}) copy-start(bf16[96,768]{1,0:T(8,128)(2,1)} %dynamic-slice_bitcast_fusion.8) | copy-start | bytes 442372
  68.6 14.6 %collective-permute-start.9 = (bf16[104,2560]{1,0:T(8,128)(2,1)S(1)}, bf16[104,2560]{1,0:T(8,128)(2,1)S(1)}, u32[]{:S(2)}, u32[]{:S(2)}) collective-permute-start(bf16[104,2560]{1,0:T(8,128)(2,1)S(1)} %pad_maximum_fusion.12), channel_id=1, source_target_pairs={{0,3},{1,0},{2,1},{3,2},{4,7},{5,4},{6,5},{7,6},{8,11},{9,8},{10,9... | collective-permute-start | bytes 1597448 | tf_op jit(solution)/shard_map/ppermute | solution.py:16
  70.7 12.5 %collective-permute-start.10 = (bf16[80,2560]{1,0:T(8,128)(2,1)S(1)}, bf16[80,2560]{1,0:T(8,128)(2,1)S(1)}, u32[]{:S(2)}, u32[]{:S(2)}) collective-permute-start(bf16[80,2560]{1,0:T(8,128)(2,1)S(1)} %slice.220), channel_id=1, source_target_pairs={{0,4},{4,0},{1,5},{5,1},{2,6},{6,2},{3,7},{7,3},{8,12},{12,8},{9,1... | collective-permute-start | bytes 1228808 | tf_op jit(solution)/shard_map/ppermute | solution.py:20
  74.6 3.1 %copy-start.13 = (bf16[128,768]{1,0:T(8,128)(2,1)S(1)}, bf16[128,768]{1,0:T(8,128)(2,1)}, u32[]{:S(2)}) copy-start(bf16[128,768]{1,0:T(8,128)(2,1)} %get-tuple-element.131) | copy-start | bytes 589828
  74.6 3.1 %copy-start.14 = (bf16[128,768]{1,0:T(8,128)(2,1)S(1)}, bf16[128,768]{1,0:T(8,128)(2,1)}, u32[]{:S(2)}) copy-start(bf16[128,768]{1,0:T(8,128)(2,1)} %get-tuple-element.132) | copy-start | bytes 589828
  76.8 27.4 %copy-start.3 = (bf16[480,2560]{1,0:T(8,128)(2,1)}, bf16[480,2560]{1,0:T(8,128)(2,1)S(1)}, u32[]{:S(2)}) copy-start(bf16[480,2560]{1,0:T(8,128)(2,1)S(1)} %convolution_convert_fusion) | copy-start | bytes 7372804
  79.5 3.9 %copy-start.5 = (bf16[384,2560]{1,0:T(8,128)(2,1)}, bf16[384,2560]{1,0:T(8,128)(2,1)S(1)}, u32[]{:S(2)}) copy-start(bf16[384,2560]{1,0:T(8,128)(2,1)S(1)} %convolution_convert_fusion.1) | copy-start | bytes 5898244
  84.5 6.4 %copy-start.8 = (bf16[1024,768]{1,0:T(8,128)(2,1)S(1)}, bf16[1024,768]{1,0:T(8,128)(2,1)}, u32[]{:S(2)}) copy-start(bf16[1024,768]{1,0:T(8,128)(2,1)} %param.8) | copy-start | bytes 4718596
  84.5 16.6 %collective-permute-start.11 = (bf16[128,2560]{1,0:T(8,128)(2,1)S(1)}, bf16[128,2560]{1,0:T(8,128)(2,1)S(1)}, u32[]{:S(2)}, u32[]{:S(2)}) collective-permute-start(bf16[128,2560]{1,0:T(8,128)(2,1)S(1)} %pad_maximum_fusion.6), channel_id=1, source_target_pairs={{0,1},{1,2},{2,3},{3,0},{4,5},{5,6},{6,7},{7,4},{8,9},{9,10},{10,1... | collective-permute-start | bytes 1966088 | tf_op jit(solution)/shard_map/ppermute | solution.py:16
  85.4 15.7 %collective-permute-start.12 = (bf16[128,2560]{1,0:T(8,128)(2,1)S(1)}, bf16[128,2560]{1,0:T(8,128)(2,1)S(1)}, u32[]{:S(2)}, u32[]{:S(2)}) collective-permute-start(bf16[128,2560]{1,0:T(8,128)(2,1)S(1)} %pad_maximum_fusion.7), channel_id=1, source_target_pairs={{0,3},{1,0},{2,1},{3,2},{4,7},{5,4},{6,5},{7,6},{8,11},{9,8},{10,9... | collective-permute-start | bytes 1966088 | tf_op jit(solution)/shard_map/ppermute | solution.py:16
  87.9 16.3 %collective-permute-start.13 = (bf16[128,2560]{1,0:T(8,128)(2,1)S(1)}, bf16[128,2560]{1,0:T(8,128)(2,1)S(1)}, u32[]{:S(2)}, u32[]{:S(2)}) collective-permute-start(bf16[128,2560]{1,0:T(8,128)(2,1)S(1)} %pad_maximum_fusion.8), channel_id=1, source_target_pairs={{0,4},{4,0},{1,5},{5,1},{2,6},{6,2},{3,7},{7,3},{8,12},{12,8},{9,1... | collective-permute-start | bytes 1966088 | tf_op jit(solution)/shard_map/ppermute | solution.py:20
  106.6 4.1 %collective-permute-start.23 = (bf16[2,8,80,768]{3,2,1,0:T(8,128)(2,1)S(1)}, bf16[2,8,80,768]{3,2,1,0:T(8,128)(2,1)S(1)}, u32[]{:S(2)}, u32[]{:S(2)}) collective-permute-start(bf16[2,8,80,768]{3,2,1,0:T(8,128)(2,1)S(1)} %fusion), channel_id=1, source_target_pairs={{0,8},{8,0},{1,9},{9,1},{2,10},{10,2},{3,11},{11,3},{4,12},{12,4},... | collective-permute-start | bytes 5898248 | tf_op jit(solution)/shard_map/ppermute | solution.py:20
  113.0 18.4 %copy-start.4 = (bf16[480,2560]{1,0:T(8,128)(2,1)S(1)}, bf16[480,2560]{1,0:T(8,128)(2,1)}, u32[]{:S(2)}) copy-start(bf16[480,2560]{1,0:T(8,128)(2,1)} %copy-done.3) | copy-start | bytes 7372804
  113.0 18.4 %collective-permute-start.14 = (bf16[128,2560]{1,0:T(8,128)(2,1)}, bf16[128,2560]{1,0:T(8,128)(2,1)}, u32[]{:S(2)}, u32[]{:S(2)}) collective-permute-start(bf16[128,2560]{1,0:T(8,128)(2,1)} %pad_maximum_fusion.9), channel_id=1, source_target_pairs={{0,1},{1,2},{2,3},{3,0},{4,5},{5,6},{6,7},{7,4},{8,9},{9,10},{10,1... | collective-permute-start | bytes 1966088 | tf_op jit(solution)/shard_map/ppermute | solution.py:16
  113.1 18.3 %collective-permute-start.15 = (bf16[128,2560]{1,0:T(8,128)(2,1)S(1)}, bf16[128,2560]{1,0:T(8,128)(2,1)}, u32[]{:S(2)}, u32[]{:S(2)}) collective-permute-start(bf16[128,2560]{1,0:T(8,128)(2,1)S(1)} %pad_maximum_fusion.10), channel_id=1, source_target_pairs={{0,3},{1,0},{2,1},{3,2},{4,7},{5,4},{6,5},{7,6},{8,11},{9,8},{10,9... | collective-permute-start | bytes 1966088 | tf_op jit(solution)/shard_map/ppermute | solution.py:16
  116.3 14.5 %collective-permute-start.16 = (bf16[96,2560]{1,0:T(8,128)(2,1)}, bf16[96,2560]{1,0:T(8,128)(2,1)}, u32[]{:S(2)}, u32[]{:S(2)}) collective-permute-start(bf16[96,2560]{1,0:T(8,128)(2,1)} %pad_maximum_fusion.13), channel_id=1, source_target_pairs={{0,4},{4,0},{1,5},{5,1},{2,6},{6,2},{3,7},{7,3},{8,12},{12,8},{9,1... | collective-permute-start | bytes 1474568 | tf_op jit(solution)/shard_map/ppermute | solution.py:20
  118.5 15.7 %copy-start.20 = (f32[2560]{0:T(1024)S(1)}, f32[2560]{0:T(1024)}, u32[]{:S(2)}) copy-start(f32[2560]{0:T(1024)} %param.12) | copy-start | bytes 30724
  118.5 15.7 %copy-start.21 = (f32[2560]{0:T(1024)S(1)}, f32[2560]{0:T(1024)}, u32[]{:S(2)}) copy-start(f32[2560]{0:T(1024)} %param.11) | copy-start | bytes 30724
  131.4 8.8 %copy-start.1 = (bf16[2,8,2,80,768]{4,3,2,1,0:T(8,128)(2,1)S(1)}, bf16[2,8,2,80,768]{4,3,2,1,0:T(8,128)(2,1)}, u32[]{:S(2)}) copy-start(bf16[2,8,2,80,768]{4,3,2,1,0:T(8,128)(2,1)} %copy-done) | copy-start | bytes 11796484
  133.8 14.3 %copy-start.2 = (bf16[128,2560]{1,0:T(8,128)(2,1)}, bf16[128,2560]{1,0:T(8,128)(2,1)S(1)}, u32[]{:S(2)}) copy-start(bf16[128,2560]{1,0:T(8,128)(2,1)S(1)} %get-tuple-element.119) | copy-start | bytes 1966084
  134.7 17.2 %collective-permute-start.17 = (bf16[128,2560]{1,0:T(8,128)(2,1)S(1)}, bf16[128,2560]{1,0:T(8,128)(2,1)S(1)}, u32[]{:S(2)}, u32[]{:S(2)}) collective-permute-start(bf16[128,2560]{1,0:T(8,128)(2,1)S(1)} %fusion.6), channel_id=1, source_target_pairs={{0,1},{1,2},{2,3},{3,0},{4,5},{5,6},{6,7},{7,4},{8,9},{9,10},{10,1... | collective-permute-start | bytes 1966088 | tf_op jit(solution)/shard_map/ppermute | solution.py:16
  134.7 17.2 %collective-permute-start.18 = (bf16[128,2560]{1,0:T(8,128)(2,1)S(1)}, bf16[128,2560]{1,0:T(8,128)(2,1)S(1)}, u32[]{:S(2)}, u32[]{:S(2)}) collective-permute-start(bf16[128,2560]{1,0:T(8,128)(2,1)S(1)} %fusion.6), channel_id=1, source_target_pairs={{0,3},{1,0},{2,1},{3,2},{4,7},{5,4},{6,5},{7,6},{8,11},{9,8},{10,9... | collective-permute-start | bytes 1966088 | tf_op jit(solution)/shard_map/ppermute | solution.py:16
  138.0 13.5 %collective-permute-start.19 = (bf16[96,2560]{1,0:T(8,128)(2,1)S(1)}, bf16[96,2560]{1,0:T(8,128)(2,1)S(1)}, u32[]{:S(2)}, u32[]{:S(2)}) collective-permute-start(bf16[96,2560]{1,0:T(8,128)(2,1)S(1)} %slice.257), channel_id=1, source_target_pairs={{0,4},{4,0},{1,5},{5,1},{2,6},{6,2},{3,7},{7,3},{8,12},{12,8},{9,1... | collective-permute-start | bytes 1474568 | tf_op jit(solution)/shard_map/ppermute | solution.py:20
  152.2 16.4 %collective-permute-start.20 = (bf16[128,2560]{1,0:T(8,128)(2,1)S(1)}, bf16[128,2560]{1,0:T(8,128)(2,1)S(1)}, u32[]{:S(2)}, u32[]{:S(2)}) collective-permute-start(bf16[128,2560]{1,0:T(8,128)(2,1)S(1)} %get-tuple-element.155), channel_id=1, source_target_pairs={{0,1},{1,2},{2,3},{3,0},{4,5},{5,6},{6,7},{7,4},{8,9},{9,10},{10,1... | collective-permute-start | bytes 1966088 | tf_op jit(solution)/shard_map/ppermute | solution.py:16
  152.9 15.8 %collective-permute-start.21 = (bf16[128,2560]{1,0:T(8,128)(2,1)S(1)}, bf16[128,2560]{1,0:T(8,128)(2,1)S(1)}, u32[]{:S(2)}, u32[]{:S(2)}) collective-permute-start(bf16[128,2560]{1,0:T(8,128)(2,1)S(1)} %get-tuple-element.154), channel_id=1, source_target_pairs={{0,3},{1,0},{2,1},{3,2},{4,7},{5,4},{6,5},{7,6},{8,11},{9,8},{10,9... | collective-permute-start | bytes 1966088 | tf_op jit(solution)/shard_map/ppermute | solution.py:16
  155.5 17.8 %collective-permute-start.22 = (bf16[128,2560]{1,0:T(8,128)(2,1)S(1)}, bf16[128,2560]{1,0:T(8,128)(2,1)S(1)}, u32[]{:S(2)}, u32[]{:S(2)}) collective-permute-start(bf16[128,2560]{1,0:T(8,128)(2,1)S(1)} %get-tuple-element.153), channel_id=1, source_target_pairs={{0,4},{4,0},{1,5},{5,1},{2,6},{6,2},{3,7},{7,3},{8,12},{12,8},{9,1... | collective-permute-start | bytes 1966088 | tf_op jit(solution)/shard_map/ppermute | solution.py:20
  157.6 21.3 %collective-permute-start.24 = (bf16[32,2560]{1,0:T(8,128)(2,1)S(1)}, bf16[32,2560]{1,0:T(8,128)(2,1)S(1)}, u32[]{:S(2)}, u32[]{:S(2)}) collective-permute-start(bf16[32,2560]{1,0:T(8,128)(2,1)S(1)} %slice.268), channel_id=1, source_target_pairs={{0,4},{4,0},{1,5},{5,1},{2,6},{6,2},{3,7},{7,3},{8,12},{12,8},{9,1... | collective-permute-start | bytes 491528 | tf_op jit(solution)/shard_map/ppermute | solution.py:20
  173.5 9.1 %collective-permute-start.26 = (bf16[64,2560]{1,0:T(8,128)(2,1)S(1)}, bf16[64,2560]{1,0:T(8,128)(2,1)S(1)}, u32[]{:S(2)}, u32[]{:S(2)}) collective-permute-start(bf16[64,2560]{1,0:T(8,128)(2,1)S(1)} %get-tuple-element.139), channel_id=1, source_target_pairs={{0,3},{1,0},{2,1},{3,2},{4,7},{5,4},{6,5},{7,6},{8,11},{9,8},{10,9... | collective-permute-start | bytes 983048 | tf_op jit(solution)/shard_map/ppermute | solution.py:16
  175.0 8.3 %collective-permute-start.25 = (bf16[64,2560]{1,0:T(8,128)(2,1)S(1)}, bf16[64,2560]{1,0:T(8,128)(2,1)S(1)}, u32[]{:S(2)}, u32[]{:S(2)}) collective-permute-start(bf16[64,2560]{1,0:T(8,128)(2,1)S(1)} %get-tuple-element.141), channel_id=1, source_target_pairs={{0,1},{1,2},{2,3},{3,0},{4,5},{5,6},{6,7},{7,4},{8,9},{9,10},{10,1... | collective-permute-start | bytes 983048 | tf_op jit(solution)/shard_map/ppermute | solution.py:16
  175.6 6.3 %collective-permute-start.27 = (f32[80,768]{1,0:T(8,128)S(1)}, f32[80,768]{1,0:T(8,128)S(1)}, u32[]{:S(2)}, u32[]{:S(2)}) collective-permute-start(f32[80,768]{1,0:T(8,128)S(1)} %dynamic-slice_bitcast_fusion), channel_id=1, source_target_pairs={{0,128},{128,0},{1,129},{129,1},{2,130},{130,2},{3,131},{131,3},{4... | collective-permute-start | bytes 737288 | tf_op jit(solution)/shard_map/ppermute | solution.py:20
  (7 other events, 10.1 us)
Sparse Core Ops, SparseCore 0:
  14.4 43.8 all-gather.2
  113.2 49.9 reduce-scatter.1

commit v3 on v2

--- a/solution.py
+++ b/solution.py
@@ -38,7 +38,7 @@
 
 def gather_second(first):
     own, left, right, side = first
-    h = own.shape[0] // 2
+    h = own.shape[0] * 9 // 16
     return send(
         jnp.concatenate([side[:h], left[:h]]),
         jnp.concatenate([side[:h], right[h:]]),
@@ -53,10 +53,10 @@
 
 def place_second(second, place):
     up, down, across = second
-    h = up.shape[0] // 2
+    h, rest = up.shape[0] // 2, across.shape[0] // 2
     place(0, 2, jnp.concatenate([up[h:], down[h:]]))
-    place(1, -1, jnp.concatenate([up[:h], across[:h]]))
-    place(1, 1, jnp.concatenate([down[:h], across[h:]]))
+    place(1, -1, jnp.concatenate([up[:h], across[:rest]]))
+    place(1, 1, jnp.concatenate([down[:h], across[rest:]]))
 
 
 class Rows:
@@ -139,7 +139,7 @@
         return lax.dynamic_slice(blocks, at, (1, 1) + blocks.shape[2:])[0, 0]
 
     middle = jnp.concatenate([block(1, 1), block(1, -1), block(0, 2)])
-    h, q, early = tok // 2, tok * 5 // 16, tok * 3 // 4
+    h, q, early = tok * 9 // 16, tok * 5 // 16, tok * 3 // 4
     side_block = block(1, 0)
     far_rows = jnp.concatenate([block(1, 2), side_block[early:]])
     near = jnp.concatenate([block(0, 1), block(0, -1), block(0, 0), side_block[:early]])
@@ -153,33 +153,30 @@
     far, second, whole_down = together((partial(far_rows), second, whole_down))
     third = send(
         jnp.concatenate([second[0][:h], far[:q]]),
-        jnp.concatenate([second[2][h:], far[q : 2 * q]]),
-        far[2 * q :],
+        jnp.concatenate([second[2][tok - h :], far[q:h]]),
+        far[h:],
     )
     place_second(second, cot.place)
     p_middle, p_near = partial(middle), partial(near)
     third, p_middle, p_near, cot_most = together((third, p_middle, p_near, cot.value))
     cot.value = cot_most
-    s_up, s_down, s_side = third[0][h:], third[1][h:], third[2][: tok - 2 * q]
+    s_up, s_down, s_side = third[0][h:], third[1][tok - h :], third[2][: tok - h]
     p_right, p_left, p_two = (p_middle[k * tok : (k + 1) * tok] for k in range(3))
     up_in = jnp.concatenate([add(p_right[:q], s_up).astype(BF16), p_right[q:h], p_two[:h]])
     down_in = jnp.concatenate(
         [
             p_left[:q],
-            add(p_left[q:h], s_down[: h - q]).astype(BF16),
-            p_two[h : 2 * q],
-            add(p_two[2 * q :], s_side).astype(BF16),
+            add(p_left[q:h], s_down).astype(BF16),
+            add(p_two[h:], s_side).astype(BF16),
         ]
     )
-    across_in = jnp.concatenate(
-        [add(p_left[h : 2 * q], s_down[h - q :]).astype(BF16), p_left[2 * q :], p_right[h:]]
-    )
+    across_in = jnp.concatenate([p_left[h:], p_right[h:]])
     up_in, down_in, across_in, third, cot.value = together(
         (up_in, down_in, across_in, third, cot.value)
     )
     up, down, across = send(up_in, down_in, across_in)
-    cot.place(1, 2, jnp.concatenate([third[0][:h], third[1][:h]]))
-    side_late = third[2][tok - 2 * q :]
+    cot.place(1, 2, jnp.concatenate([third[0][:h], third[1][: tok - h]]))
+    side_late = third[2][tok - h :]
     cot_all = cot.value
     grad = lax.dot_general(
         cot_all.reshape(-1, width), hidden, (((0,), (0,)), ((), ())), preferred_element_type=F32
@@ -187,9 +184,9 @@
     up, down, across, p_near, grad, cot_all = together((up, down, across, p_near, grad, cot_all))
     q_right, q_left, q_own = (p_near[k * tok : (k + 1) * tok] for k in range(3))
     q_side = p_near[3 * tok :]
-    right_in = jnp.concatenate([add(q_right[:h], up[h:]), add(q_right[h:], across[h:])])
+    right_in = jnp.concatenate([add(q_right[:h], up[h:]), add(q_right[h:], across[tok - h :])])
     left_in = jnp.concatenate(
-        [q_left[:h], add(q_left[h:], down[h:], across[:h]).astype(BF16)]
+        [q_left[:h], add(q_left[h:], down[h:], across[: tok - h]).astype(BF16)]
     )
     side_in = jnp.concatenate([add(q_side[:h], up[:h], down[:h]).astype(BF16), q_side[h:]])
     right_in, left_in, side_in, grad = together((right_in.astype(BF16), left_in, side_in, grad))
@@ -212,11 +209,11 @@
     first, grad_hidden, cot_all = together((first, grad_hidden, cot_all))
     normed = Rows(cot_all)
     second = gather_second(first)
+    second, grad_chips, first = together((second, grad_chips, first))
+    up, _, across = second
+    third = send(up[:h], across[tok - h :], first[0][early:])
+    summed = scatter_low(grad_chips)
     place_first(first, normed.place)
-    second, grad_chips = together((second, grad_chips))
-    up, _, across = second
-    third = send(up[:h], across[h:], first[0][early:])
-    summed = scatter_low(grad_chips)
     place_second(second, normed.place)
     normed.place(1, 0, jnp.concatenate([first[3], third[2]]))
     normed.place(1, 2, jnp.concatenate([third[0], third[1]]))

time: 191 us -> 195 us (1.021)
  waiting for transfers between devices: 73.8 us -> 71.2 us
  other arithmetic: 19.5 us -> 21.5 us
  local copies, waits for them, and re-layouts: 17.1 us -> 19.1 us
  starting transfers between devices: 45.3 us -> 47.3 us
    ppermute x16, waiting for transfers between devices: 27.8 us -> 14.7 us  [shift_x(): return lax.ppermute(v, 'x', [(i, (i + s) % NX) for i in range(NX)])]
    ppermute x12, waiting for transfers between devices: 40.5 us -> 50.4 us  [swap(): return lax.ppermute(v, axis, [(0, 1), (1, 0)])]
    concatenate x5 -> x8, other arithmetic: 1.05 us -> 3.11 us  [the longest x2 1.08 us: gather_second(): jnp.concatenate([side[:h], left[:h]])]
  transfers between devices with their start and end apart: 30 -> 30, of which waited for: 20 -> 18; matrix products, arithmetic and copies ran while one was open for 23% -> 23% of each run, Pallas kernels for 0% -> 0%
where the time goes in v3:
time: 195 us
  waiting for transfers between devices  71.2 us (37%)
  starting transfers between devices  47.3 us (24%)
  other arithmetic  21.5 us (11%)
  matrix products  19.5 us (10%)
  local copies, waits for them, and re-layouts  19.1 us (10%)
  between operations  16 us (8%)
    ppermute x12, waiting for transfers between devices, swap(): return lax.ppermute(v, axis, [(0, 1), (1, 0)])  50.4 us
    ppermute x16, starting transfers between devices, shift_x(): return lax.ppermute(v, 'x', [(i, (i + s) % NX) for i in range(NX)])  25.8 us
    ppermute x12, starting transfers between devices, swap(): return lax.ppermute(v, axis, [(0, 1), (1, 0)])  21.5 us
    ppermute x16, waiting for transfers between devices, shift_x(): return lax.ppermute(v, 'x', [(i, (i + s) % NX) for i in range(NX)])  14.7 us
    dynamic_update_slice x9, other arithmetic, place(): self.value = lax.dynamic_update_slice(self.value, block[None, None], at)  7.96 us
    dot_general x1, matrix products, body(): jnp.dot(cot_all.reshape(-1, width), whole_down, preferred_element_type=F32)  7.89 us
    dot_general x1, matrix products, body(): lax.dot_general(cot_all.reshape(-1, width), hidden, (((0,), (0,)), ((), (...  6.38 us
    dynamic_update_slice x7, local copies, waits for them, and re-layouts, place(): self.value = lax.dynamic_update_slice(self.value, block[None, None], at)  6.23 us
  transfers between devices with their start and end apart: 30, of which 18 were waited for; matrix products, arithmetic and copies ran while one was open for 23% of the time, Pallas kernels for 0%

profile of v3, /device:TPU:8, one launch (start us, length us, event | category | flops | bytes accessed | tf_op | source)
XLA Modules:
  0.0 194.7 jit_solution(6898933990907858348)
XLA Ops:
  7.2 2.3 %collective-permute-start = (bf16[80,768]{1,0:T(8,128)(2,1)}, bf16[80,768]{1,0:T(8,128)(2,1)S(1)}, u32[]{:S(2)}, u32[]{:S(2)}) collective-permute-start(bf16[80,768]{1,0:T(8,128)(2,1)} %param.9), channel_id=1, source_target_pairs={{0,128},{128,0},{1,129},{129,1},{2,130},{130,2},{3,131},{131,3},{4... | collective-permute-start | bytes 368648 | tf_op jit(solution)/shard_map/ppermute | solution.py:20
  9.5 1.3 dynamic_slice.41
  14.4 1.6 collective-permute-start.1
  16.0 1.7 collective-permute-start.2
  17.7 2.3 %collective-permute-start.3 = (bf16[128,2560]{1,0:T(8,128)(2,1)S(1)}, bf16[128,2560]{1,0:T(8,128)(2,1)S(1)}, u32[]{:S(2)}, u32[]{:S(2)}) collective-permute-start(bf16[128,2560]{1,0:T(8,128)(2,1)S(1)} %multiply_convert_fusion), channel_id=1, source_target_pairs={{0,4},{4,0},{1,5},{5,1},{2,6},{6,2},{3,7},{7,3},{8,12},{12,8},{9,1... | collective-permute-start | bytes 1966088 | tf_op jit(solution)/shard_map/ppermute | solution.py:20
  20.0 11.1 %collective-permute-done.1 = bf16[128,2560]{1,0:T(8,128)(2,1)S(1)} collective-permute-done((bf16[128,2560]{1,0:T(8,128)(2,1)S(1)}, bf16[128,2560]{1,0:T(8,128)(2,1)S(1)}, u32[]{:S(2)}, u32[]{:S(2)}) %collective-permute-start.1) | collective-permute-done | bytes 655392 | tf_op jit(solution)/shard_map/ppermute | solution.py:16
  31.3 2.9 %collective-permute-done.3 = bf16[128,2560]{1,0:T(8,128)(2,1)S(1)} collective-permute-done((bf16[128,2560]{1,0:T(8,128)(2,1)S(1)}, bf16[128,2560]{1,0:T(8,128)(2,1)S(1)}, u32[]{:S(2)}, u32[]{:S(2)}) %collective-permute-start.3) | collective-permute-done | bytes 655392 | tf_op jit(solution)/shard_map/ppermute | solution.py:20
  34.9 2.9 %collective-permute-start.5 = (bf16[128,2560]{1,0:T(8,128)(2,1)S(1)}, bf16[128,2560]{1,0:T(8,128)(2,1)S(1)}, u32[]{:S(2)}, u32[]{:S(2)}) collective-permute-start(bf16[128,2560]{1,0:T(8,128)(2,1)S(1)} %pad_maximum_fusion.3), channel_id=1, source_target_pairs={{0,3},{1,0},{2,1},{3,2},{4,7},{5,4},{6,5},{7,6},{8,11},{9,8},{10,9... | collective-permute-start | bytes 1966088 | tf_op jit(solution)/shard_map/ppermute | solution.py:16
  37.8 2.5 %collective-permute-start.6 = (bf16[112,2560]{1,0:T(8,128)(2,1)S(1)}, bf16[112,2560]{1,0:T(8,128)(2,1)S(1)}, u32[]{:S(2)}, u32[]{:S(2)}) collective-permute-start(bf16[112,2560]{1,0:T(8,128)(2,1)S(1)} %pad_maximum_fusion.8), channel_id=1, source_target_pairs={{0,4},{4,0},{1,5},{5,1},{2,6},{6,2},{3,7},{7,3},{8,12},{12,8},{9,1... | collective-permute-start | bytes 1720328 | tf_op jit(solution)/shard_map/ppermute | solution.py:20
  41.0 1.0 dynamic-slice_bitcast_fusion.3
  42.1 2.8 %broadcast_in_dim.55 = bf16[2,4,128,2560]{3,2,1,0:T(8,128)(2,1)} broadcast(bf16[]{:T(256)} %constant.44.clone.1), dimensions={} | broadcast | bytes 5242882 | tf_op jit(solution)/shard_map/broadcast_in_dim | solution.py:128
  45.8 5.4 %collective-permute-done.6 = bf16[112,2560]{1,0:T(8,128)(2,1)S(1)} collective-permute-done((bf16[112,2560]{1,0:T(8,128)(2,1)S(1)}, bf16[112,2560]{1,0:T(8,128)(2,1)S(1)}, u32[]{:S(2)}, u32[]{:S(2)}) %collective-permute-start.6) | collective-permute-done | bytes 573472 | tf_op jit(solution)/shard_map/ppermute | solution.py:20
  51.9 6.0 %all-gather.3.cloned.1.call-done = bf16[16,80,768]{2,1,0:T(8,128)(2,1)} async-done(((bf16[2,80,768]{2,1,0:T(8,128)(2,1)}), bf16[16,80,768]{2,1,0:T(8,128)(2,1)}) %all-gather.3.cloned.1.call-update) | async-done | bytes 1966096 | tf_op jit(solution)/shard_map/all_gather | solution.py:124
  60.6 1.5 collective-permute-done.7
  63.2 1.4 convolution_convert_fusion.2
  64.7 1.4 fusion.37
  66.2 1.9 collective-permute-start.8
  68.2 2.0 %collective-permute-start.9 = (bf16[88,2560]{1,0:T(8,128)(2,1)S(1)}, bf16[88,2560]{1,0:T(8,128)(2,1)S(1)}, u32[]{:S(2)}, u32[]{:S(2)}) collective-permute-start(bf16[88,2560]{1,0:T(8,128)(2,1)S(1)} %pad_maximum_fusion.13), channel_id=1, source_target_pairs={{0,3},{1,0},{2,1},{3,2},{4,7},{5,4},{6,5},{7,6},{8,11},{9,8},{10,9... | collective-permute-start | bytes 1351688 | tf_op jit(solution)/shard_map/ppermute | solution.py:16
  70.2 2.1 %collective-permute-start.10 = (bf16[88,2560]{1,0:T(8,128)(2,1)S(1)}, bf16[88,2560]{1,0:T(8,128)(2,1)S(1)}, u32[]{:S(2)}, u32[]{:S(2)}) collective-permute-start(bf16[88,2560]{1,0:T(8,128)(2,1)S(1)} %slice.206), channel_id=1, source_target_pairs={{0,4},{4,0},{1,5},{5,1},{2,6},{6,2},{3,7},{7,3},{8,12},{12,8},{9,1... | collective-permute-start | bytes 1351688 | tf_op jit(solution)/shard_map/ppermute | solution.py:20
  74.1 2.1 %convolution_convert_fusion = bf16[480,2560]{1,0:T(8,128)(2,1)S(1)} fusion(bf16[2560,768]{1,0:T(8,128)(2,1)S(1)} %bitcast.105, bf16[96,768]{1,0:T(8,128)(2,1)S(1)} %copy-done.25, bf16[128,768]{1,0:T(8,128)(2,1)S(1)} %copy-done.23, bf16[128,768]{1,0:T(8,128)(2,1)S(1)} %copy-done.24, bf16[128,768]{1,0:T(8,128)(2,1)S(1)} %copy-done.22), kind=kOutput, calls=%fused_computation | convolution fusion | flops 1891614720 | bytes 7127040 | tf_op jit(solution)/shard_map/dot_general | solution.py:149
  77.2 1.7 convolution_convert_fusion.1
  78.9 1.5 collective-permute-done.9
  80.4 3.4 %collective-permute-done.10 = bf16[88,2560]{1,0:T(8,128)(2,1)S(1)} collective-permute-done((bf16[88,2560]{1,0:T(8,128)(2,1)S(1)}, bf16[88,2560]{1,0:T(8,128)(2,1)S(1)}, u32[]{:S(2)}, u32[]{:S(2)}) %collective-permute-start.10) | collective-permute-done | bytes 450592 | tf_op jit(solution)/shard_map/ppermute | solution.py:20
  85.8 3.2 %collective-permute-start.12 = (bf16[128,2560]{1,0:T(8,128)(2,1)S(1)}, bf16[128,2560]{1,0:T(8,128)(2,1)S(1)}, u32[]{:S(2)}, u32[]{:S(2)}) collective-permute-start(bf16[128,2560]{1,0:T(8,128)(2,1)S(1)} %pad_maximum_fusion.4), channel_id=1, source_target_pairs={{0,3},{1,0},{2,1},{3,2},{4,7},{5,4},{6,5},{7,6},{8,11},{9,8},{10,9... | collective-permute-start | bytes 1966088 | tf_op jit(solution)/shard_map/ppermute | solution.py:16
  89.0 2.1 %collective-permute-start.13 = (bf16[112,2560]{1,0:T(8,128)(2,1)S(1)}, bf16[112,2560]{1,0:T(8,128)(2,1)S(1)}, u32[]{:S(2)}, u32[]{:S(2)}) collective-permute-start(bf16[112,2560]{1,0:T(8,128)(2,1)S(1)} %pad_maximum_fusion.10), channel_id=1, source_target_pairs={{0,4},{4,0},{1,5},{5,1},{2,6},{6,2},{3,7},{7,3},{8,12},{12,8},{9,1... | collective-permute-start | bytes 1720328 | tf_op jit(solution)/shard_map/ppermute | solution.py:20
  92.1 6.4 %fusion.40 = f32[2560,768]{1,0:T(8,128)S(1)} fusion(bf16[1024,2560]{1,0:T(8,128)(2,1)} %bitcast.26, bf16[1024,768]{1,0:T(8,128)(2,1)S(1)} %copy-done.11), kind=kOutput, calls=%fused_computation.106 | convolution fusion | flops 4026531840 | bytes 14680064 | tf_op jit(solution)/shard_map/dot_general | solution.py:181
  98.5 5.4 %collective-permute-done.13 = bf16[112,2560]{1,0:T(8,128)(2,1)S(1)} collective-permute-done((bf16[112,2560]{1,0:T(8,128)(2,1)S(1)}, bf16[112,2560]{1,0:T(8,128)(2,1)S(1)}, u32[]{:S(2)}, u32[]{:S(2)}) %collective-permute-start.13) | collective-permute-done | bytes 573472 | tf_op jit(solution)/shard_map/ppermute | solution.py:20
  105.7 1.0 pad_maximum_fusion.5
  106.9 4.0 %collective-permute-done.23 = bf16[2,8,80,768]{3,2,1,0:T(8,128)(2,1)S(1)} collective-permute-done((bf16[2,8,80,768]{3,2,1,0:T(8,128)(2,1)S(1)}, bf16[2,8,80,768]{3,2,1,0:T(8,128)(2,1)S(1)}, u32[]{:S(2)}, u32[]{:S(2)}) %collective-permute-start.23) | collective-permute-done | bytes 1966112 | tf_op jit(solution)/shard_map/ppermute | solution.py:20
  110.9 2.3 %bitcast_add_fusion = f32[2,8,80,768]{3,2,1,0:T(8,128)} fusion(bf16[2,8,80,768]{3,2,1,0:T(8,128)(2,1)S(1)} %collective-permute-done.23, f32[2,8,2,80,768]{4,3,2,1,0:T(8,128)S(1)} %bitcast.110, u32[]{:T(128)S(6)} %convert_element_type.148), kind=kLoop, calls=%fused_computation.3 | loop fusion | flops 1966080 | bytes 9830404 | tf_op jit(solution)/shard_map/add | solution.py:113
  113.4 3.2 %collective-permute-start.15 = (bf16[128,2560]{1,0:T(8,128)(2,1)S(1)}, bf16[128,2560]{1,0:T(8,128)(2,1)S(1)}, u32[]{:S(2)}, u32[]{:S(2)}) collective-permute-start(bf16[128,2560]{1,0:T(8,128)(2,1)S(1)} %get-tuple-element.100), channel_id=1, source_target_pairs={{0,3},{1,0},{2,1},{3,2},{4,7},{5,4},{6,5},{7,6},{8,11},{9,8},{10,9... | collective-permute-start | bytes 1966088 | tf_op jit(solution)/shard_map/ppermute | solution.py:16
  116.6 2.1 %collective-permute-start.16 = (bf16[96,2560]{1,0:T(8,128)(2,1)}, bf16[96,2560]{1,0:T(8,128)(2,1)S(1)}, u32[]{:S(2)}, u32[]{:S(2)}) collective-permute-start(bf16[96,2560]{1,0:T(8,128)(2,1)} %pad_maximum_fusion.12), channel_id=1, source_target_pairs={{0,4},{4,0},{1,5},{5,1},{2,6},{6,2},{3,7},{7,3},{8,12},{12,8},{9,1... | collective-permute-start | bytes 1474568 | tf_op jit(solution)/shard_map/ppermute | solution.py:20
  118.7 0.9 slice.239
  119.6 11.4 %collective-permute-done.16 = bf16[96,2560]{1,0:T(8,128)(2,1)S(1)} collective-permute-done((bf16[96,2560]{1,0:T(8,128)(2,1)}, bf16[96,2560]{1,0:T(8,128)(2,1)S(1)}, u32[]{:S(2)}, u32[]{:S(2)}) %collective-permute-start.16) | collective-permute-done | bytes 491552 | tf_op jit(solution)/shard_map/ppermute | solution.py:20
  131.6 1.8 convert_reduce_fusion
  134.3 3.2 %collective-permute-start.18 = (bf16[128,2560]{1,0:T(8,128)(2,1)S(1)}, bf16[128,2560]{1,0:T(8,128)(2,1)S(1)}, u32[]{:S(2)}, u32[]{:S(2)}) collective-permute-start(bf16[128,2560]{1,0:T(8,128)(2,1)S(1)} %fusion.6), channel_id=1, source_target_pairs={{0,3},{1,0},{2,1},{3,2},{4,7},{5,4},{6,5},{7,6},{8,11},{9,8},{10,9... | collective-permute-start | bytes 1966088 | tf_op jit(solution)/shard_map/ppermute | solution.py:16
  137.6 2.2 %collective-permute-start.19 = (bf16[96,2560]{1,0:T(8,128)(2,1)S(1)}, bf16[96,2560]{1,0:T(8,128)(2,1)S(1)}, u32[]{:S(2)}, u32[]{:S(2)}) collective-permute-start(bf16[96,2560]{1,0:T(8,128)(2,1)S(1)} %slice.240), channel_id=1, source_target_pairs={{0,4},{4,0},{1,5},{5,1},{2,6},{6,2},{3,7},{7,3},{8,12},{12,8},{9,1... | collective-permute-start | bytes 1474568 | tf_op jit(solution)/shard_map/ppermute | solution.py:20
  139.8 7.9 %convolution_convert_fusion.3 = bf16[1024,768]{1,0:T(8,128)(2,1)} fusion(bf16[1024,2560]{1,0:T(8,128)(2,1)} %bitcast.27, bf16[2560,768]{1,0:T(8,128)(2,1)S(1)} %bitcast.107), kind=kOutput, calls=%fused_computation.9 | convolution fusion | flops 4027318272 | bytes 10747904 | tf_op jit(solution)/shard_map/dot_general | solution.py:206
  147.7 3.5 %collective-permute-done.19 = bf16[96,2560]{1,0:T(8,128)(2,1)S(1)} collective-permute-done((bf16[96,2560]{1,0:T(8,128)(2,1)S(1)}, bf16[96,2560]{1,0:T(8,128)(2,1)S(1)}, u32[]{:S(2)}, u32[]{:S(2)}) %collective-permute-start.19) | collective-permute-done | bytes 491552 | tf_op jit(solution)/shard_map/ppermute | solution.py:20
  151.6 1.0 pad_maximum_fusion.2
  154.1 2.7 %collective-permute-start.21 = (bf16[128,2560]{1,0:T(8,128)(2,1)}, bf16[128,2560]{1,0:T(8,128)(2,1)S(1)}, u32[]{:S(2)}, u32[]{:S(2)}) collective-permute-start(bf16[128,2560]{1,0:T(8,128)(2,1)} %pad_maximum_fusion.7), channel_id=1, source_target_pairs={{0,3},{1,0},{2,1},{3,2},{4,7},{5,4},{6,5},{7,6},{8,11},{9,8},{10,9... | collective-permute-start | bytes 1966088 | tf_op jit(solution)/shard_map/ppermute | solution.py:16
  157.7 2.1 %collective-permute-start.22 = (bf16[112,2560]{1,0:T(8,128)(2,1)}, bf16[112,2560]{1,0:T(8,128)(2,1)S(1)}, u32[]{:S(2)}, u32[]{:S(2)}) collective-permute-start(bf16[112,2560]{1,0:T(8,128)(2,1)} %pad_maximum_fusion.11), channel_id=1, source_target_pairs={{0,4},{4,0},{1,5},{5,1},{2,6},{6,2},{3,7},{7,3},{8,12},{12,8},{9,1... | collective-permute-start | bytes 1720328 | tf_op jit(solution)/shard_map/ppermute | solution.py:20
  159.8 12.5 %collective-permute-done.22 = bf16[112,2560]{1,0:T(8,128)(2,1)S(1)} collective-permute-done((bf16[112,2560]{1,0:T(8,128)(2,1)}, bf16[112,2560]{1,0:T(8,128)(2,1)S(1)}, u32[]{:S(2)}, u32[]{:S(2)}) %collective-permute-start.22) | collective-permute-done | bytes 573472 | tf_op jit(solution)/shard_map/ppermute | solution.py:20
  172.4 1.0 bitcast_dynamic-update-slice_fusion.2
  173.3 1.2 fusion.36
  174.7 2.2 %collective-permute-start.24 = (bf16[32,2560]{1,0:T(8,128)(2,1)S(1)}, bf16[32,2560]{1,0:T(8,128)(2,1)S(1)}, u32[]{:S(2)}, u32[]{:S(2)}) collective-permute-start(bf16[32,2560]{1,0:T(8,128)(2,1)S(1)} %slice.251), channel_id=1, source_target_pairs={{0,4},{4,0},{1,5},{5,1},{2,6},{6,2},{3,7},{7,3},{8,12},{12,8},{9,1... | collective-permute-start | bytes 491528 | tf_op jit(solution)/shard_map/ppermute | solution.py:20
  176.8 1.4 collective-permute-start.26
  178.9 1.5 collective-permute-start.27
  (167 shorter events, 29.6 us)
Async XLA Ops:
  7.2 7.1 %copy-start.14 = (bf16[128,2560]{1,0:T(8,128)(2,1)S(1)}, bf16[128,2560]{1,0:T(8,128)(2,1)}, u32[]{:S(2)}) copy-start(bf16[128,2560]{1,0:T(8,128)(2,1)} %param.15) | copy-start | bytes 1966084
  7.2 50.8 %all-gather.3.cloned.1.call-start = ((), (), s32[]{:S(2)}) async-start(), calls=%async_computation.2 | async-start | bytes 2211840 | tf_op jit(solution)/shard_map/all_gather | solution.py:124
  7.2 5.4 %collective-permute-start = (bf16[80,768]{1,0:T(8,128)(2,1)}, bf16[80,768]{1,0:T(8,128)(2,1)S(1)}, u32[]{:S(2)}, u32[]{:S(2)}) collective-permute-start(bf16[80,768]{1,0:T(8,128)(2,1)} %param.9), channel_id=1, source_target_pairs={{0,128},{128,0},{1,129},{129,1},{2,130},{130,2},{3,131},{131,3},{4... | collective-permute-start | bytes 368648 | tf_op jit(solution)/shard_map/ppermute | solution.py:20
  14.2 158.1 %reduce-scatter.2.cloned.1.call-start = ((), (), s32[]{:S(2)}) async-start(), calls=%async_computation.1 | async-start | bytes 4423680 | tf_op jit(solution)/shard_map/reduce_scatter | solution.py:95
  14.4 16.7 %collective-permute-start.1 = (bf16[128,2560]{1,0:T(8,128)(2,1)S(1)}, bf16[128,2560]{1,0:T(8,128)(2,1)S(1)}, u32[]{:S(2)}, u32[]{:S(2)}) collective-permute-start(bf16[128,2560]{1,0:T(8,128)(2,1)S(1)} %multiply_convert_fusion), channel_id=1, source_target_pairs={{0,1},{1,2},{2,3},{3,0},{4,5},{5,6},{6,7},{7,4},{8,9},{9,10},{10,1... | collective-permute-start | bytes 1966088 | tf_op jit(solution)/shard_map/ppermute | solution.py:16
  16.0 15.3 %collective-permute-start.2 = (bf16[128,2560]{1,0:T(8,128)(2,1)S(1)}, bf16[128,2560]{1,0:T(8,128)(2,1)S(1)}, u32[]{:S(2)}, u32[]{:S(2)}) collective-permute-start(bf16[128,2560]{1,0:T(8,128)(2,1)S(1)} %multiply_convert_fusion), channel_id=1, source_target_pairs={{0,3},{1,0},{2,1},{3,2},{4,7},{5,4},{6,5},{7,6},{8,11},{9,8},{10,9... | collective-permute-start | bytes 1966088 | tf_op jit(solution)/shard_map/ppermute | solution.py:16
  17.7 16.4 %collective-permute-start.3 = (bf16[128,2560]{1,0:T(8,128)(2,1)S(1)}, bf16[128,2560]{1,0:T(8,128)(2,1)S(1)}, u32[]{:S(2)}, u32[]{:S(2)}) collective-permute-start(bf16[128,2560]{1,0:T(8,128)(2,1)S(1)} %multiply_convert_fusion), channel_id=1, source_target_pairs={{0,4},{4,0},{1,5},{5,1},{2,6},{6,2},{3,7},{7,3},{8,12},{12,8},{9,1... | collective-permute-start | bytes 1966088 | tf_op jit(solution)/shard_map/ppermute | solution.py:20
  34.3 6.0 %copy-start.10 = (bf16[1024,768]{1,0:T(8,128)(2,1)S(1)}, bf16[1024,768]{1,0:T(8,128)(2,1)}, u32[]{:S(2)}) copy-start(bf16[1024,768]{1,0:T(8,128)(2,1)} %param.8) | copy-start | bytes 4718596
  34.3 17.6 %collective-permute-start.4 = (bf16[144,2560]{1,0:T(8,128)(2,1)S(1)}, bf16[144,2560]{1,0:T(8,128)(2,1)}, u32[]{:S(2)}, u32[]{:S(2)}) collective-permute-start(bf16[144,2560]{1,0:T(8,128)(2,1)S(1)} %pad_maximum_fusion), channel_id=1, source_target_pairs={{0,1},{1,2},{2,3},{3,0},{4,5},{5,6},{6,7},{7,4},{8,9},{9,10},{10,1... | collective-permute-start | bytes 2211848 | tf_op jit(solution)/shard_map/ppermute | solution.py:16
  34.9 16.3 %collective-permute-start.5 = (bf16[128,2560]{1,0:T(8,128)(2,1)S(1)}, bf16[128,2560]{1,0:T(8,128)(2,1)S(1)}, u32[]{:S(2)}, u32[]{:S(2)}) collective-permute-start(bf16[128,2560]{1,0:T(8,128)(2,1)S(1)} %pad_maximum_fusion.3), channel_id=1, source_target_pairs={{0,3},{1,0},{2,1},{3,2},{4,7},{5,4},{6,5},{7,6},{8,11},{9,8},{10,9... | collective-permute-start | bytes 1966088 | tf_op jit(solution)/shard_map/ppermute | solution.py:16
  37.8 13.3 %collective-permute-start.6 = (bf16[112,2560]{1,0:T(8,128)(2,1)S(1)}, bf16[112,2560]{1,0:T(8,128)(2,1)S(1)}, u32[]{:S(2)}, u32[]{:S(2)}) collective-permute-start(bf16[112,2560]{1,0:T(8,128)(2,1)S(1)} %pad_maximum_fusion.8), channel_id=1, source_target_pairs={{0,4},{4,0},{1,5},{5,1},{2,6},{6,2},{3,7},{7,3},{8,12},{12,8},{9,1... | collective-permute-start | bytes 1720328 | tf_op jit(solution)/shard_map/ppermute | solution.py:20
  44.9 13.1 %copy-start.5 = (bf16[128,2560]{1,0:T(8,128)(2,1)S(1)}, bf16[128,2560]{1,0:T(8,128)(2,1)}, u32[]{:S(2)}) copy-start(bf16[128,2560]{1,0:T(8,128)(2,1)} %copy-done.4) | copy-start | bytes 1966084
  51.9 12.8 %copy-start.13 = (bf16[128,2560]{1,0:T(8,128)(2,1)}, bf16[128,2560]{1,0:T(8,128)(2,1)S(1)}, u32[]{:S(2)}) copy-start(bf16[128,2560]{1,0:T(8,128)(2,1)S(1)} %collective-permute-done.5) | copy-start | bytes 1966084
  57.9 4.2 %collective-permute-start.7 = (bf16[8,2,80,768]{3,2,1,0:T(8,128)(2,1)}, bf16[8,2,80,768]{3,2,1,0:T(8,128)(2,1)S(1)}, u32[]{:S(2)}, u32[]{:S(2)}) collective-permute-start(bf16[8,2,80,768]{3,2,1,0:T(8,128)(2,1)} %bitcast.111), channel_id=1, source_target_pairs={{0,8},{8,0},{1,9},{9,1},{2,10},{10,2},{3,11},{11,3},{4,12},{12,4},... | collective-permute-start | bytes 5898248 | tf_op jit(solution)/shard_map/ppermute | solution.py:20
  63.2 14.0 %copy-start = (bf16[2,8,2,80,768]{4,3,2,1,0:T(8,128)(2,1)}, bf16[2,8,2,80,768]{4,3,2,1,0:T(8,128)(2,1)S(1)}, u32[]{:S(2)}) copy-start(bf16[2,8,2,80,768]{4,3,2,1,0:T(8,128)(2,1)S(1)} %copy.14) | copy-start | bytes 11796484
  66.1 6.2 %slice-start.6 = ((bf16[128,2560]{1,0:T(8,128)(2,1)}), bf16[56,2560]{1,0:T(8,128)(2,1)S(1)}, s32[]{:S(2)}) async-start(bf16[128,2560]{1,0:T(8,128)(2,1)} %copy-done.13), calls=%async_computation.9 | async-start | bytes 573440 | tf_op jit(solution)/shard_map/slice | solution.py:57
  66.2 17.6 %collective-permute-start.8 = (bf16[112,2560]{1,0:T(8,128)(2,1)S(1)}, bf16[112,2560]{1,0:T(8,128)(2,1)S(1)}, u32[]{:S(2)}, u32[]{:S(2)}) collective-permute-start(bf16[112,2560]{1,0:T(8,128)(2,1)S(1)} %pad_maximum_fusion.9), channel_id=1, source_target_pairs={{0,1},{1,2},{2,3},{3,0},{4,5},{5,6},{6,7},{7,4},{8,9},{9,10},{10,1... | collective-permute-start | bytes 1720328 | tf_op jit(solution)/shard_map/ppermute | solution.py:16
  68.1 6.0 %copy-start.22 = (bf16[128,768]{1,0:T(8,128)(2,1)S(1)}, bf16[128,768]{1,0:T(8,128)(2,1)}, u32[]{:S(2)}) copy-start(bf16[128,768]{1,0:T(8,128)(2,1)} %get-tuple-element.136) | copy-start | bytes 589828
  68.1 6.0 %copy-start.23 = (bf16[128,768]{1,0:T(8,128)(2,1)S(1)}, bf16[128,768]{1,0:T(8,128)(2,1)}, u32[]{:S(2)}) copy-start(bf16[128,768]{1,0:T(8,128)(2,1)} %get-tuple-element.137) | copy-start | bytes 589828
  68.1 6.0 %copy-start.24 = (bf16[128,768]{1,0:T(8,128)(2,1)S(1)}, bf16[128,768]{1,0:T(8,128)(2,1)}, u32[]{:S(2)}) copy-start(bf16[128,768]{1,0:T(8,128)(2,1)} %get-tuple-element.138) | copy-start | bytes 589828
  68.1 6.0 %copy-start.25 = (bf16[96,768]{1,0:T(8,128)(2,1)S(1)}, bf16[96,768]{1,0:T(8,128)(2,1)}, u32[]{:S(2)}) copy-start(bf16[96,768]{1,0:T(8,128)(2,1)} %dynamic-slice_bitcast_fusion.8) | copy-start | bytes 442372
  68.2 12.2 %collective-permute-start.9 = (bf16[88,2560]{1,0:T(8,128)(2,1)S(1)}, bf16[88,2560]{1,0:T(8,128)(2,1)S(1)}, u32[]{:S(2)}, u32[]{:S(2)}) collective-permute-start(bf16[88,2560]{1,0:T(8,128)(2,1)S(1)} %pad_maximum_fusion.13), channel_id=1, source_target_pairs={{0,3},{1,0},{2,1},{3,2},{4,7},{5,4},{6,5},{7,6},{8,11},{9,8},{10,9... | collective-permute-start | bytes 1351688 | tf_op jit(solution)/shard_map/ppermute | solution.py:16
  70.2 13.6 %collective-permute-start.10 = (bf16[88,2560]{1,0:T(8,128)(2,1)S(1)}, bf16[88,2560]{1,0:T(8,128)(2,1)S(1)}, u32[]{:S(2)}, u32[]{:S(2)}) collective-permute-start(bf16[88,2560]{1,0:T(8,128)(2,1)S(1)} %slice.206), channel_id=1, source_target_pairs={{0,4},{4,0},{1,5},{5,1},{2,6},{6,2},{3,7},{7,3},{8,12},{12,8},{9,1... | collective-permute-start | bytes 1351688 | tf_op jit(solution)/shard_map/ppermute | solution.py:20
  78.9 5.8 %copy-start.8 = (bf16[384,2560]{1,0:T(8,128)(2,1)}, bf16[384,2560]{1,0:T(8,128)(2,1)S(1)}, u32[]{:S(2)}) copy-start(bf16[384,2560]{1,0:T(8,128)(2,1)S(1)} %convolution_convert_fusion.1) | copy-start | bytes 5898244
  85.7 6.4 %copy-start.11 = (bf16[1024,768]{1,0:T(8,128)(2,1)S(1)}, bf16[1024,768]{1,0:T(8,128)(2,1)}, u32[]{:S(2)}) copy-start(bf16[1024,768]{1,0:T(8,128)(2,1)} %param.8) | copy-start | bytes 4718596
  85.7 18.7 %collective-permute-start.11 = (bf16[144,2560]{1,0:T(8,128)(2,1)S(1)}, bf16[144,2560]{1,0:T(8,128)(2,1)S(1)}, u32[]{:S(2)}, u32[]{:S(2)}) collective-permute-start(bf16[144,2560]{1,0:T(8,128)(2,1)S(1)} %pad_maximum_fusion.1), channel_id=1, source_target_pairs={{0,1},{1,2},{2,3},{3,0},{4,5},{5,6},{6,7},{7,4},{8,9},{9,10},{10,1... | collective-permute-start | bytes 2211848 | tf_op jit(solution)/shard_map/ppermute | solution.py:16
  85.8 18.0 %collective-permute-start.12 = (bf16[128,2560]{1,0:T(8,128)(2,1)S(1)}, bf16[128,2560]{1,0:T(8,128)(2,1)S(1)}, u32[]{:S(2)}, u32[]{:S(2)}) collective-permute-start(bf16[128,2560]{1,0:T(8,128)(2,1)S(1)} %pad_maximum_fusion.4), channel_id=1, source_target_pairs={{0,3},{1,0},{2,1},{3,2},{4,7},{5,4},{6,5},{7,6},{8,11},{9,8},{10,9... | collective-permute-start | bytes 1966088 | tf_op jit(solution)/shard_map/ppermute | solution.py:16
  89.0 14.8 %collective-permute-start.13 = (bf16[112,2560]{1,0:T(8,128)(2,1)S(1)}, bf16[112,2560]{1,0:T(8,128)(2,1)S(1)}, u32[]{:S(2)}, u32[]{:S(2)}) collective-permute-start(bf16[112,2560]{1,0:T(8,128)(2,1)S(1)} %pad_maximum_fusion.10), channel_id=1, source_target_pairs={{0,4},{4,0},{1,5},{5,1},{2,6},{6,2},{3,7},{7,3},{8,12},{12,8},{9,1... | collective-permute-start | bytes 1720328 | tf_op jit(solution)/shard_map/ppermute | solution.py:20
  106.8 4.1 %collective-permute-start.23 = (bf16[2,8,80,768]{3,2,1,0:T(8,128)(2,1)S(1)}, bf16[2,8,80,768]{3,2,1,0:T(8,128)(2,1)S(1)}, u32[]{:S(2)}, u32[]{:S(2)}) collective-permute-start(bf16[2,8,80,768]{3,2,1,0:T(8,128)(2,1)S(1)} %fusion), channel_id=1, source_target_pairs={{0,8},{8,0},{1,9},{9,1},{2,10},{10,2},{3,11},{11,3},{4,12},{12,4},... | collective-permute-start | bytes 5898248 | tf_op jit(solution)/shard_map/ppermute | solution.py:20
  113.3 18.3 %collective-permute-start.14 = (bf16[128,2560]{1,0:T(8,128)(2,1)}, bf16[128,2560]{1,0:T(8,128)(2,1)S(1)}, u32[]{:S(2)}, u32[]{:S(2)}) collective-permute-start(bf16[128,2560]{1,0:T(8,128)(2,1)} %get-tuple-element.99), channel_id=1, source_target_pairs={{0,1},{1,2},{2,3},{3,0},{4,5},{5,6},{6,7},{7,4},{8,9},{9,10},{10,1... | collective-permute-start | bytes 1966088 | tf_op jit(solution)/shard_map/ppermute | solution.py:16
  113.4 18.2 %collective-permute-start.15 = (bf16[128,2560]{1,0:T(8,128)(2,1)S(1)}, bf16[128,2560]{1,0:T(8,128)(2,1)S(1)}, u32[]{:S(2)}, u32[]{:S(2)}) collective-permute-start(bf16[128,2560]{1,0:T(8,128)(2,1)S(1)} %get-tuple-element.100), channel_id=1, source_target_pairs={{0,3},{1,0},{2,1},{3,2},{4,7},{5,4},{6,5},{7,6},{8,11},{9,8},{10,9... | collective-permute-start | bytes 1966088 | tf_op jit(solution)/shard_map/ppermute | solution.py:16
  116.6 14.4 %collective-permute-start.16 = (bf16[96,2560]{1,0:T(8,128)(2,1)}, bf16[96,2560]{1,0:T(8,128)(2,1)S(1)}, u32[]{:S(2)}, u32[]{:S(2)}) collective-permute-start(bf16[96,2560]{1,0:T(8,128)(2,1)} %pad_maximum_fusion.12), channel_id=1, source_target_pairs={{0,4},{4,0},{1,5},{5,1},{2,6},{6,2},{3,7},{7,3},{8,12},{12,8},{9,1... | collective-permute-start | bytes 1474568 | tf_op jit(solution)/shard_map/ppermute | solution.py:20
  119.6 14.1 %copy-start.26 = (f32[2560]{0:T(1024)S(1)}, f32[2560]{0:T(1024)}, u32[]{:S(2)}) copy-start(f32[2560]{0:T(1024)} %param.12) | copy-start | bytes 30724
  119.6 14.1 %copy-start.27 = (f32[2560]{0:T(1024)S(1)}, f32[2560]{0:T(1024)}, u32[]{:S(2)}) copy-start(f32[2560]{0:T(1024)} %param.11) | copy-start | bytes 30724
  131.6 8.2 %copy-start.1 = (bf16[2,8,2,80,768]{4,3,2,1,0:T(8,128)(2,1)S(1)}, bf16[2,8,2,80,768]{4,3,2,1,0:T(8,128)(2,1)}, u32[]{:S(2)}) copy-start(bf16[2,8,2,80,768]{4,3,2,1,0:T(8,128)(2,1)} %copy-done) | copy-start | bytes 11796484
  133.4 14.3 %copy-start.2 = (bf16[128,2560]{1,0:T(8,128)(2,1)}, bf16[128,2560]{1,0:T(8,128)(2,1)S(1)}, u32[]{:S(2)}) copy-start(bf16[128,2560]{1,0:T(8,128)(2,1)S(1)} %get-tuple-element.127) | copy-start | bytes 1966084
  134.2 17.3 %collective-permute-start.17 = (bf16[128,2560]{1,0:T(8,128)(2,1)S(1)}, bf16[128,2560]{1,0:T(8,128)(2,1)S(1)}, u32[]{:S(2)}, u32[]{:S(2)}) collective-permute-start(bf16[128,2560]{1,0:T(8,128)(2,1)S(1)} %fusion.6), channel_id=1, source_target_pairs={{0,1},{1,2},{2,3},{3,0},{4,5},{5,6},{6,7},{7,4},{8,9},{9,10},{10,1... | collective-permute-start | bytes 1966088 | tf_op jit(solution)/shard_map/ppermute | solution.py:16
  134.3 17.3 %collective-permute-start.18 = (bf16[128,2560]{1,0:T(8,128)(2,1)S(1)}, bf16[128,2560]{1,0:T(8,128)(2,1)S(1)}, u32[]{:S(2)}, u32[]{:S(2)}) collective-permute-start(bf16[128,2560]{1,0:T(8,128)(2,1)S(1)} %fusion.6), channel_id=1, source_target_pairs={{0,3},{1,0},{2,1},{3,2},{4,7},{5,4},{6,5},{7,6},{8,11},{9,8},{10,9... | collective-permute-start | bytes 1966088 | tf_op jit(solution)/shard_map/ppermute | solution.py:16
  137.6 13.6 %collective-permute-start.19 = (bf16[96,2560]{1,0:T(8,128)(2,1)S(1)}, bf16[96,2560]{1,0:T(8,128)(2,1)S(1)}, u32[]{:S(2)}, u32[]{:S(2)}) collective-permute-start(bf16[96,2560]{1,0:T(8,128)(2,1)S(1)} %slice.240), channel_id=1, source_target_pairs={{0,4},{4,0},{1,5},{5,1},{2,6},{6,2},{3,7},{7,3},{8,12},{12,8},{9,1... | collective-permute-start | bytes 1474568 | tf_op jit(solution)/shard_map/ppermute | solution.py:20
  152.7 19.7 %collective-permute-start.20 = (bf16[144,2560]{1,0:T(8,128)(2,1)}, bf16[144,2560]{1,0:T(8,128)(2,1)}, u32[]{:S(2)}, u32[]{:S(2)}) collective-permute-start(bf16[144,2560]{1,0:T(8,128)(2,1)} %pad_maximum_fusion.2), channel_id=1, source_target_pairs={{0,1},{1,2},{2,3},{3,0},{4,5},{5,6},{6,7},{7,4},{8,9},{9,10},{10,1... | collective-permute-start | bytes 2211848 | tf_op jit(solution)/shard_map/ppermute | solution.py:16
  154.1 18.2 %collective-permute-start.21 = (bf16[128,2560]{1,0:T(8,128)(2,1)}, bf16[128,2560]{1,0:T(8,128)(2,1)S(1)}, u32[]{:S(2)}, u32[]{:S(2)}) collective-permute-start(bf16[128,2560]{1,0:T(8,128)(2,1)} %pad_maximum_fusion.7), channel_id=1, source_target_pairs={{0,3},{1,0},{2,1},{3,2},{4,7},{5,4},{6,5},{7,6},{8,11},{9,8},{10,9... | collective-permute-start | bytes 1966088 | tf_op jit(solution)/shard_map/ppermute | solution.py:16
  157.7 14.6 %collective-permute-start.22 = (bf16[112,2560]{1,0:T(8,128)(2,1)}, bf16[112,2560]{1,0:T(8,128)(2,1)S(1)}, u32[]{:S(2)}, u32[]{:S(2)}) collective-permute-start(bf16[112,2560]{1,0:T(8,128)(2,1)} %pad_maximum_fusion.11), channel_id=1, source_target_pairs={{0,4},{4,0},{1,5},{5,1},{2,6},{6,2},{3,7},{7,3},{8,12},{12,8},{9,1... | collective-permute-start | bytes 1720328 | tf_op jit(solution)/shard_map/ppermute | solution.py:20
  173.3 7.1 %copy-start.7 = (bf16[128,2560]{1,0:T(8,128)(2,1)S(1)}, bf16[128,2560]{1,0:T(8,128)(2,1)}, u32[]{:S(2)}) copy-start(bf16[128,2560]{1,0:T(8,128)(2,1)} %copy-done.6) | copy-start | bytes 1966084
  174.6 7.6 %slice-start.4 = ((bf16[128,2560]{1,0:T(8,128)(2,1)}), bf16[56,2560]{1,0:T(8,128)(2,1)S(1)}, s32[]{:S(2)}) async-start(bf16[128,2560]{1,0:T(8,128)(2,1)} %copy-done.12), calls=%async_computation.7 | async-start | bytes 573440 | tf_op jit(solution)/shard_map/slice | solution.py:57
  174.7 10.2 %collective-permute-start.24 = (bf16[32,2560]{1,0:T(8,128)(2,1)S(1)}, bf16[32,2560]{1,0:T(8,128)(2,1)S(1)}, u32[]{:S(2)}, u32[]{:S(2)}) collective-permute-start(bf16[32,2560]{1,0:T(8,128)(2,1)S(1)} %slice.251), channel_id=1, source_target_pairs={{0,4},{4,0},{1,5},{5,1},{2,6},{6,2},{3,7},{7,3},{8,12},{12,8},{9,1... | collective-permute-start | bytes 491528 | tf_op jit(solution)/shard_map/ppermute | solution.py:20
  176.8 9.6 %collective-permute-start.26 = (bf16[56,2560]{1,0:T(8,128)(2,1)S(1)}, bf16[56,2560]{1,0:T(8,128)(2,1)S(1)}, u32[]{:S(2)}, u32[]{:S(2)}) collective-permute-start(bf16[56,2560]{1,0:T(8,128)(2,1)S(1)} %get-tuple-element.147), channel_id=1, source_target_pairs={{0,3},{1,0},{2,1},{3,2},{4,7},{5,4},{6,5},{7,6},{8,11},{9,8},{10,9... | collective-permute-start | bytes 860168 | tf_op jit(solution)/shard_map/ppermute | solution.py:16
  178.2 8.7 %collective-permute-start.25 = (bf16[72,2560]{1,0:T(8,128)(2,1)S(1)}, bf16[72,2560]{1,0:T(8,128)(2,1)S(1)}, u32[]{:S(2)}, u32[]{:S(2)}) collective-permute-start(bf16[72,2560]{1,0:T(8,128)(2,1)S(1)} %get-tuple-element.143), channel_id=1, source_target_pairs={{0,1},{1,2},{2,3},{3,0},{4,5},{5,6},{6,7},{7,4},{8,9},{9,10},{10,1... | collective-permute-start | bytes 1105928 | tf_op jit(solution)/shard_map/ppermute | solution.py:16
  178.9 6.8 %collective-permute-start.27 = (f32[80,768]{1,0:T(8,128)S(1)}, f32[80,768]{1,0:T(8,128)S(1)}, u32[]{:S(2)}, u32[]{:S(2)}) collective-permute-start(f32[80,768]{1,0:T(8,128)S(1)} %dynamic-slice_bitcast_fusion), channel_id=1, source_target_pairs={{0,128},{128,0},{1,129},{129,1},{2,130},{130,2},{3,131},{131,3},{4... | collective-permute-start | bytes 737288 | tf_op jit(solution)/shard_map/ppermute | solution.py:20
  (18 other events, 44.5 us)
Sparse Core Ops, SparseCore 0:
  14.4 43.5 all-gather.2
  113.4 49.5 reduce-scatter.1
